TPU v7x, 128 devices: a whole 4x4x4 slice. The times are simulated.
128 devices in a mesh: lat: 2 (over z_lo), lon: 64 (over x, y, z_hi, core).
Axes of the slice: x: 4, y: 4, z: 4 (z_hi: 2, z_lo: 2; z = z_hi * 2 + z_lo), core: 2. Of those that a mesh axis runs over, the one named last changes fastest.
Arguments:
- grid_state: bfloat16 [84, 32, 8192], P(None, 'lat', 'lon'), may hold values from -6 to 6
- mesh_feat: bfloat16 [32768, 1024], P(('lat', 'lon')), may hold values from -6 to 6
- enc_src: int32 [16, 32768], P(None, ('lat', 'lon')), may hold values from 0 to 5119, as said below
- enc_count: int32 [32768], P(('lat', 'lon')), may hold values from 1 to 16, as said below
- nbr_ids: int32 [32, 32768], P(None, ('lat', 'lon')), may hold values from 0 to 32767, as said below
- nbr_count: int32 [32768], P(('lat', 'lon')), may hold values from 2 to 32, as said below
- dec_src: int32 [3, 32, 8192], P(None, 'lat', 'lon'), may hold values from 0 to 32767, as said below
- w_embed: bfloat16 [84, 1024], replicated, may hold values from -0.625 to 0.625
- w_encode: bfloat16 [1024, 1024], replicated, may hold values from -0.1875 to 0.1875
- w_query: bfloat16 [1024, 1024], replicated, may hold values from -4 to 4
- w_key: bfloat16 [1024, 1024], replicated, may hold values from -4 to 4
- w_value: bfloat16 [1024, 1024], replicated, may hold values from -0.1875 to 0.1875
- w_output: bfloat16 [1024, 1024], replicated, may hold values from -0.1875 to 0.1875
- w_decode: bfloat16 [1024, 1024], replicated, may hold values from -0.1875 to 0.1875
- w_readout: bfloat16 [1024, 84], replicated, may hold values from -0.1875 to 0.1875
- norm_attn: float32 [1024], replicated, may hold values from 0.5 to 1.5
- norm_dec: float32 [1024], replicated, may hold values from 0.5 to 1.5
Outputs:
- denoised: float32 [84, 32, 8192], P(None, 'lat', 'lon')
Inputs may be any that keep to these rules, and one draw needn't show every extreme that they name: `enc_src`: mesh node j belongs to block j // 256, numbered lat index times the number of lon indices plus lon index. Every entry of column j, padding included, names a cell of the window of 160 columns around that lon index's sector, in any row. `enc_count`: some node of every block has 16. `nbr_ids`: slot 0 of node j is j itself. The 32 slots of a node, padding included, are distinct mesh nodes whose block has the same or a cyclically adjacent lon index, and any lat index. `nbr_count`: some node of every block has 32. `dec_src`: the mesh nodes feeding cell (r, c) lie in blocks whose lon index is c // 128 or cyclically adjacent to it, any lat index.
All inputs are finite; a program needn't handle non-finite values.
Results may differ from a plain program's by a relative error of at most 0.0039.
Values may be sent and summed in bfloat16 or wider, within the bound.
A program may use at most 128 MiB of HBM per device.

v0:
```python
import jax
import jax.numpy as jnp
from jax import lax
from jax.sharding import PartitionSpec as P

HEADS = 16
HALO = 16
KM = 32


def with_halo(block, sides, width):
    for axis, dim in sides:
        count = lax.axis_size(axis)
        forward = [(i, i + 1) for i in range(count - 1)]
        forward.append((count - 1, 0))
        backward = [(target, source) for source, target in forward]
        low = lax.ppermute(
            lax.slice_in_dim(block, block.shape[dim] - width, None, axis=dim), axis, forward
        )
        high = lax.ppermute(lax.slice_in_dim(block, 0, width, axis=dim), axis, backward)
        block = jnp.concatenate([low, block, high], axis=dim)
    return block


def from_everyone(array, axis):
    copies = jnp.broadcast_to(array, (lax.axis_size(axis), *array.shape))
    return lax.all_to_all(copies, axis, split_axis=0, concat_axis=0, tiled=True)


def joined_along(blocks, dim):
    blocks = jnp.moveaxis(blocks, 0, dim)
    lengths = blocks.shape
    return blocks.reshape(*lengths[:dim], lengths[dim] * lengths[dim + 1], *lengths[dim + 2 :])


def collect(array, axis, dim):
    blocks = from_everyone(array, axis)
    return joined_along(blocks, dim)


def passed_along(value, axis, steps):
    count = lax.axis_size(axis)
    pairs = [(source, (source + steps) % count) for source in range(count)]
    return lax.ppermute(value, axis, pairs)


def layer_norm(inputs_f, gain):
    centre = inputs_f - jnp.mean(inputs_f, axis=-1, keepdims=True)
    spread = jnp.mean(centre * centre, axis=-1, keepdims=True)
    return centre * lax.rsqrt(spread + 1e-05) * gain


def window_index(global_ids, node_count, lon_count, sector):
    device = global_ids // node_count
    band_index = device // lon_count
    offset = (device % lon_count - sector + 1) % lon_count
    return (band_index * 3 + offset) * node_count + global_ids % node_count


def arrange(from_west, own_part, from_east, node_count, axis_pos):
    full_shape = own_part.shape
    band_count = full_shape[axis_pos] // node_count
    parted = full_shape[:axis_pos] + (band_count, 1, node_count) + full_shape[axis_pos + 1 :]
    joined = jnp.concatenate(
        [from_west.reshape(parted), own_part.reshape(parted), from_east.reshape(parted)],
        axis=axis_pos + 1,
    )
    return joined.reshape(
        full_shape[:axis_pos] + (band_count * 3 * node_count,) + full_shape[axis_pos + 1 :]
    )


def body(
    grid_state,
    mesh_feat,
    enc_src,
    enc_count,
    nbr_ids,
    nbr_count,
    dec_src,
    w_embed,
    w_encode,
    w_query,
    w_key,
    w_value,
    w_output,
    w_decode,
    w_readout,
    norm_attn,
    norm_dec,
):
    lon_count = lax.axis_size("lon")
    sector = lax.axis_index("lon")
    variables, lat_rows, lon_cols = grid_state.shape
    node_count, feature_count = mesh_feat.shape
    head_count = HEADS
    head_width = feature_count // head_count
    padded = with_halo(grid_state, (("lon", 2),), HALO)
    grid_window = lax.all_gather(padded, "lat", axis=1, tiled=True)
    flat_grid = grid_window.reshape(variables, -1)
    picked = jnp.take(flat_grid, enc_src, axis=1).astype(jnp.float32)
    live_edge = lax.broadcasted_iota(jnp.int32, enc_src.shape, 0) < enc_count[None, :]
    summed = jnp.sum(jnp.where(live_edge[None], picked, 0.0), axis=1)
    mean_cells = (summed / enc_count.astype(jnp.float32)[None, :]).astype(jnp.bfloat16)
    embedded = jax.nn.silu(
        lax.dot_general(
            mean_cells, w_embed, (((0,), (0,)), ((), ())), preferred_element_type=jnp.float32
        )
    ).astype(jnp.bfloat16)
    latent = mesh_feat.astype(jnp.float32) + jnp.dot(
        embedded, w_encode, preferred_element_type=jnp.float32
    )
    normed = layer_norm(latent, norm_attn).astype(jnp.bfloat16)
    queries = jnp.dot(normed, w_query, preferred_element_type=jnp.float32).astype(jnp.bfloat16)
    banded = collect(normed, "lat", 0)
    from_west = passed_along(banded, "lon", 1)
    from_east = passed_along(banded, "lon", -1)
    normed_window = arrange(from_west, banded, from_east, node_count, 0)
    key_window = jnp.dot(normed_window, w_key, preferred_element_type=jnp.float32).astype(
        jnp.bfloat16
    )
    value_window = jnp.dot(normed_window, w_value, preferred_element_type=jnp.float32).astype(
        jnp.bfloat16
    )
    window_rows = key_window.shape[0]
    neighbour = window_index(nbr_ids, node_count, lon_count, sector)
    live_slot = lax.broadcasted_iota(jnp.int32, nbr_ids.shape, 0) < nbr_count[None, :]
    block_rows = min(node_count, 512)
    blocks = node_count // block_rows
    score_scale = head_width ** (-0.5)
    query_blocks = queries.reshape(blocks, block_rows, head_count, head_width)
    index_blocks = neighbour.reshape(KM, blocks, block_rows).transpose(1, 0, 2)
    live_blocks = live_slot.reshape(KM, blocks, block_rows).transpose(1, 0, 2)
    key_heads = key_window.reshape(window_rows, head_count, head_width)
    value_heads = value_window.reshape(window_rows, head_count, head_width)

    def attend(operands):
        query_block, index_block, live_block = operands
        row_ids = lax.broadcasted_iota(jnp.int32, index_block.shape, 1)
        member = jnp.zeros((block_rows, window_rows), jnp.int32)
        member = member.at[row_ids, index_block].max(live_block.astype(jnp.int32)) > 0

        def one_head(head_index):
            query_head = lax.dynamic_index_in_dim(query_block, head_index, 1, False)
            key_head = lax.dynamic_index_in_dim(key_heads, head_index, 1, False)
            value_head = lax.dynamic_index_in_dim(value_heads, head_index, 1, False)
            scores = (
                lax.dot_general(
                    query_head,
                    key_head,
                    (((1,), (1,)), ((), ())),
                    preferred_element_type=jnp.float32,
                )
                * score_scale
            )
            scores = jnp.where(member, scores, -jnp.inf)
            peak_score = jnp.max(scores, axis=1, keepdims=True)
            expo_score = jnp.where(member, jnp.exp(scores - peak_score), 0.0)
            weights = (expo_score / jnp.sum(expo_score, axis=1, keepdims=True)).astype(jnp.bfloat16)
            return jnp.dot(weights, value_head, preferred_element_type=jnp.float32).astype(
                jnp.bfloat16
            )

        per_head = lax.map(one_head, jnp.arange(head_count, dtype=jnp.int32))
        return per_head.transpose(1, 0, 2).reshape(block_rows, feature_count)

    context = lax.map(attend, (query_blocks, index_blocks, live_blocks)).reshape(
        node_count, feature_count
    )
    mixed = latent + jnp.dot(context, w_output, preferred_element_type=jnp.float32)
    normed_out = layer_norm(mixed, norm_dec).astype(jnp.bfloat16)
    decoded = jax.nn.silu(jnp.dot(normed_out, w_decode, preferred_element_type=jnp.float32)).astype(
        jnp.bfloat16
    )
    local_read = lax.dot_general(
        w_readout, decoded, (((0,), (1,)), ((), ())), preferred_element_type=jnp.float32
    ).astype(jnp.bfloat16)
    banded = lax.all_gather(local_read, "lat", axis=1, tiled=True)
    from_west = passed_along(banded, "lon", 1)
    from_east = passed_along(banded, "lon", -1)
    readout = arrange(from_west, banded, from_east, node_count, 1)
    targets = window_index(dec_src, node_count, lon_count, sector)
    picked_out = jnp.take(readout, targets.reshape(-1), axis=1).reshape(
        variables, 3, lat_rows, lon_cols
    )
    update = jnp.sum(picked_out.astype(jnp.float32), axis=1) / 3.0
    return grid_state.astype(jnp.float32) + update


def solution(mesh):
    in_specs = (
        P(None, "lat", "lon"),
        P(("lat", "lon"), None),
        P(None, ("lat", "lon")),
        P(("lat", "lon")),
        P(None, ("lat", "lon")),
        P(("lat", "lon")),
        P(None, "lat", "lon"),
        P(),
        P(),
        P(),
        P(),
        P(),
        P(),
        P(),
        P(),
        P(),
        P(),
    )
    out_specs = P(None, "lat", "lon")
    return jax.shard_map(body, mesh=mesh, in_specs=in_specs, out_specs=out_specs, check_vma=False)
```

profile of v0, /device:TPU:87, one launch (start us, length us, event | category | flops | bytes accessed | tf_op | source)
XLA Modules:
  0.0 314.0 jit_solution(7747262814465791211)
XLA Ops:
  8.6 45.4 %scatter_custom_fusion = s32[393216]{0:T(1024)} fusion(s32[8192]{0:T(1024)S(1)} %bitcast.83, s32[8192]{0:T(1024)S(1)} %bitcast.84, s32[]{:T(128)} %constant.173.clone.1), kind=kCustom, calls=%fused_computation.37 | custom fusion | flops 8192 | bytes 1572868
  55.4 15.9 %all_gather.6 = bf16[84,32,160]{2,1,0:T(8,128)(2,1)} all-gather(bf16[84,16,160]{2,1,0:T(8,128)(2,1)S(1)} %pad_maximum_fusion.1), channel_id=1, replica_groups=mesh['lat'=2,'lon'=64] {'lat'}, dimensions={1}, use_global_device_ids=true | all-gather | bytes 1290240 | tf_op jit(solution)/shard_map/all_gather | solution.py:99
  71.3 2.7 copy.30
  74.0 14.9 %gather_fusion = bf16[4096,84]{1,0:T(8,128)(2,1)} fusion(bf16[84,5120]{0,1:T(8,128)(2,1)S(1)} %bitcast.73, s32[4096]{0:T(1024)S(1)} %broadcast_clamp_fusion.1), kind=kCustom, calls=%fused_computation | custom fusion | bytes 1392640 | tf_op jit(solution)/shard_map/jit(_take)/gather | solution.py:101
  88.9 3.0 select_reduce_fusion
  91.9 2.8 fusion.54
  97.2 4.4 %all-to-all-start = ((bf16[2,256,1024]{2,1,0:T(8,128)(2,1)}), bf16[2,256,1024]{2,1,0:T(8,128)(2,1)}, u32[]{:S(2)}, u32[]{:S(2)}) async-start(bf16[2,256,1024]{2,1,0:T(8,128)(2,1)} %broadcast_in_dim.76), calls=%async_computation | async-start | bytes 2097152 | tf_op jit(solution)/shard_map/all_to_all | solution.py:27
  101.6 2.4 broadcast_compare_fusion
  104.0 2.0 reshape.171
  107.4 4.9 %all-to-all-done = bf16[2,256,1024]{2,1,0:T(8,128)(2,1)} async-done(((bf16[2,256,1024]{2,1,0:T(8,128)(2,1)}), bf16[2,256,1024]{2,1,0:T(8,128)(2,1)}, u32[]{:S(2)}, u32[]{:S(2)}) %all-to-all-start) | async-done | bytes 1048608 | tf_op jit(solution)/shard_map/all_to_all | solution.py:27
  112.3 4.1 %collective-permute-start.3 = (bf16[512,1024]{1,0:T(8,128)(2,1)}, bf16[512,1024]{1,0:T(8,128)(2,1)}, u32[]{:S(2)}, u32[]{:S(2)}) collective-permute-start(bf16[512,1024]{1,0:T(8,128)(2,1)} %bitcast.8), channel_id=1, source_target_pairs={{0,63},{1,0},{2,1},{3,2},{4,3},{5,4},{6,5},{7,6},{8,7},{9,8},{10,9... | collective-permute-start | bytes 3145736 | tf_op jit(solution)/shard_map/ppermute | solution.py:44
  116.4 15.6 %collective-permute-start.2 = (bf16[512,1024]{1,0:T(8,128)(2,1)}, bf16[512,1024]{1,0:T(8,128)(2,1)}, u32[]{:S(2)}, u32[]{:S(2)}) collective-permute-start(bf16[512,1024]{1,0:T(8,128)(2,1)} %bitcast.8), channel_id=1, source_target_pairs={{0,1},{1,2},{2,3},{3,4},{4,5},{5,6},{6,7},{7,8},{8,9},{9,10},{10,1... | collective-permute-start | bytes 3145736 | tf_op jit(solution)/shard_map/ppermute | solution.py:44
  133.4 3.3 %convolution_convert_fusion.3 = bf16[256,1024]{1,0:T(8,128)(2,1)} fusion(bf16[256,1024]{1,0:T(8,128)(2,1)} %copy-done.4, bf16[1024,1024]{1,0:T(8,128)(2,1)} %param.28), kind=kOutput, calls=%fused_computation.27 | convolution fusion | flops 537133056 | bytes 3145728 | tf_op jit(solution)/shard_map/dot_general | solution.py:114
  136.7 2.1 copy.31
  138.8 6.1 %collective-permute-done.3 = bf16[512,1024]{1,0:T(8,128)(2,1)} collective-permute-done((bf16[512,1024]{1,0:T(8,128)(2,1)}, bf16[512,1024]{1,0:T(8,128)(2,1)}, u32[]{:S(2)}, u32[]{:S(2)}) %collective-permute-start.3) | collective-permute-done | bytes 1048608 | tf_op jit(solution)/shard_map/ppermute | solution.py:44
  144.8 2.2 pad_maximum_fusion
  147.1 5.0 %convolution_convert_fusion.2 = bf16[1536,1024]{0,1:T(8,128)(2,1)} fusion(bf16[1536,1024]{1,0:T(8,128)(2,1)S(1)} %bitcast.75, bf16[1024,1024]{1,0:T(8,128)(2,1)S(1)} %copy-done), kind=kOutput, calls=%fused_computation.21 | convolution fusion | flops 3222798336 | bytes 8388608 | tf_op jit(solution)/shard_map/dot_general | solution.py:119
  152.1 5.0 %convolution_convert_fusion.1 = bf16[1536,1024]{0,1:T(8,128)(2,1)} fusion(bf16[1536,1024]{1,0:T(8,128)(2,1)S(1)} %bitcast.76, bf16[1024,1024]{1,0:T(8,128)(2,1)S(1)} %copy-done.10), kind=kOutput, calls=%fused_computation.20 | convolution fusion | flops 3222798336 | bytes 8388608 | tf_op jit(solution)/shard_map/dot_general | solution.py:122
  157.1 105.8 %while.17 = (s32[]{:T(128)}, bf16[16,256,64]{1,2,0:T(8,128)(2,1)}, s32[16]{0:T(128)S(1)}, bf16[256,16,64]{0,2,1:T(8,128)(2,1)}, bf16[1536,16,64]{0,2,1:T(8,128)(...) while((s32[]{:T(128)}, bf16[16,256,64]{1,2,0:T(8,128)(2,1)}, ...), condition=%wide.region_7.8_spmd, body=%wide.region_4.7_spmd.sunk | while | flops 104611328 | bytes 6363799 | solution.py:164
  161.6 2.2 fusion.75
  168.2 2.2 fusion.75
  172.8 1.5 fusion.73
  174.8 2.2 fusion.75
  179.4 1.5 fusion.73
  181.4 2.2 fusion.75
  188.0 2.2 fusion.75
  192.7 1.5 fusion.73
  194.6 2.2 fusion.75
  199.3 1.5 fusion.73
  201.2 2.2 fusion.75
  207.8 2.2 fusion.75
  214.5 2.2 fusion.75
  221.1 2.2 fusion.75
  227.7 2.2 fusion.75
  234.3 2.2 fusion.75
  240.9 2.2 fusion.75
  247.5 2.2 fusion.75
  254.1 2.2 fusion.75
  260.7 2.2 fusion.75
  262.9 2.6 fusion.55
  266.8 2.9 fusion.13
  269.7 4.2 %all_gather.7 = bf16[84,512]{1,0:T(8,128)(2,1)S(1)} all-gather(bf16[84,256]{1,0:T(8,128)(2,1)S(1)} %fusion.13), channel_id=1, replica_groups=mesh['lat'=2,'lon'=64] {'lat'}, dimensions={1}, use_global_device_ids=true | all-gather | bytes 129024 | tf_op jit(solution)/shard_map/all_gather | solution.py:178
  273.9 4.6 %collective-permute-start.4 = (bf16[84,512]{1,0:T(8,128)(2,1)S(1)}, bf16[84,512]{1,0:T(8,128)(2,1)S(1)}, u32[]{:S(2)}, u32[]{:S(2)}) collective-permute-start(bf16[84,512]{1,0:T(8,128)(2,1)S(1)} %all_gather.7), channel_id=1, source_target_pairs={{0,1},{1,2},{2,3},{3,4},{4,5},{5,6},{6,7},{7,8},{8,9},{9,10},{10,1... | collective-permute-start | bytes 258056 | tf_op jit(solution)/shard_map/ppermute | solution.py:44
  278.6 1.5 collective-permute-done.4
  280.1 4.8 %collective-permute-done.5 = bf16[84,512]{1,0:T(8,128)(2,1)S(1)} collective-permute-done((bf16[84,512]{1,0:T(8,128)(2,1)S(1)}, bf16[84,512]{1,0:T(8,128)(2,1)S(1)}, u32[]{:S(2)}, u32[]{:S(2)}) %collective-permute-start.5) | collective-permute-done | bytes 86048 | tf_op jit(solution)/shard_map/ppermute | solution.py:44
  285.7 22.1 %gather_fusion.1 = bf16[6144,84]{1,0:T(8,128)(2,1)} fusion(bf16[84,1536]{0,1:T(8,128)(2,1)S(1)} %bitcast.72, s32[6144]{0:T(1024)S(1)} %broadcast_clamp_fusion), kind=kCustom, calls=%fused_computation.1 | custom fusion | bytes 2088960 | tf_op jit(solution)/shard_map/jit(_take)/gather | solution.py:183
  307.7 3.0 convert_reduce_fusion
  312.0 2.0 multiply_add_fusion
  (110 shorter events, 53.6 us)
Async XLA Ops:
  0.0 147.0 %copy-start = (bf16[1024,1024]{1,0:T(8,128)(2,1)S(1)}, bf16[1024,1024]{1,0:T(8,128)(2,1)}, u32[]{:S(2)}) copy-start(bf16[1024,1024]{1,0:T(8,128)(2,1)} %param.29) | copy-start | bytes 6291460
  0.0 54.0 %copy-start.1 = (bf16[84,16,128]{2,1,0:T(8,128)(2,1)S(1)}, bf16[84,16,128]{2,1,0:T(8,128)(2,1)}, u32[]{:S(2)}) copy-start(bf16[84,16,128]{2,1,0:T(8,128)(2,1)} %param.19) | copy-start | bytes 1032196
  1.4 52.6 %collective-permute-start = (bf16[84,16,16]{2,1,0:T(8,128)(2,1)S(1)}, bf16[84,16,16]{2,1,0:T(8,128)(2,1)S(1)}, u32[]{:S(2)}, u32[]{:S(2)}) collective-permute-start(bf16[84,16,16]{2,1,0:T(8,128)(2,1)S(1)} %get-tuple-element.89), channel_id=1, source_target_pairs={{0,1},{1,2},{2,3},{3,4},{4,5},{5,6},{6,7},{7,8},{8,9},{9,10},{10,1... | collective-permute-start | bytes 129032 | tf_op jit(solution)/shard_map/ppermute | solution.py:17
  2.1 51.9 %collective-permute-start.1 = (bf16[84,16,16]{2,1,0:T(8,128)(2,1)S(1)}, bf16[84,16,16]{2,1,0:T(8,128)(2,1)}, u32[]{:S(2)}, u32[]{:S(2)}) collective-permute-start(bf16[84,16,16]{2,1,0:T(8,128)(2,1)S(1)} %get-tuple-element.90), channel_id=1, source_target_pairs={{1,0},{2,1},{3,2},{4,3},{5,4},{6,5},{7,6},{8,7},{9,8},{10,9},{11,1... | collective-permute-start | bytes 129032 | tf_op jit(solution)/shard_map/ppermute | solution.py:20
  74.0 14.9 %copy-start.6 = (pred[16,256]{1,0:T(8,128)(4,1)S(1)}, pred[16,256]{1,0:T(8,128)(4,1)}, u32[]{:S(2)}) copy-start(pred[16,256]{1,0:T(8,128)(4,1)} %get-tuple-element.95) | copy-start | bytes 12292
  74.0 14.9 %copy-start.7 = (pred[16,256]{1,0:T(8,128)(4,1)S(1)}, pred[16,256]{1,0:T(8,128)(4,1)}, u32[]{:S(2)}) copy-start(pred[16,256]{1,0:T(8,128)(4,1)} %get-tuple-element.96) | copy-start | bytes 12292
  74.0 17.9 %copy-start.9 = (f32[256]{0:T(256)S(1)}, f32[256]{0:T(256)}, u32[]{:S(2)}) copy-start(f32[256]{0:T(256)} %convert_element_type.58) | copy-start | bytes 3076
  91.9 3.1 copy-start.8
  95.3 0.8 copy-start.4
  97.2 15.1 %all-to-all-start = ((bf16[2,256,1024]{2,1,0:T(8,128)(2,1)}), bf16[2,256,1024]{2,1,0:T(8,128)(2,1)}, u32[]{:S(2)}, u32[]{:S(2)}) async-start(bf16[2,256,1024]{2,1,0:T(8,128)(2,1)} %broadcast_in_dim.76), calls=%async_computation | async-start | bytes 2097152 | tf_op jit(solution)/shard_map/all_to_all | solution.py:27
  112.3 32.5 %collective-permute-start.3 = (bf16[512,1024]{1,0:T(8,128)(2,1)}, bf16[512,1024]{1,0:T(8,128)(2,1)}, u32[]{:S(2)}, u32[]{:S(2)}) collective-permute-start(bf16[512,1024]{1,0:T(8,128)(2,1)} %bitcast.8), channel_id=1, source_target_pairs={{0,63},{1,0},{2,1},{3,2},{4,3},{5,4},{6,5},{7,6},{8,7},{9,8},{10,9... | collective-permute-start | bytes 3145736 | tf_op jit(solution)/shard_map/ppermute | solution.py:44
  116.4 28.4 %collective-permute-start.2 = (bf16[512,1024]{1,0:T(8,128)(2,1)}, bf16[512,1024]{1,0:T(8,128)(2,1)}, u32[]{:S(2)}, u32[]{:S(2)}) collective-permute-start(bf16[512,1024]{1,0:T(8,128)(2,1)} %bitcast.8), channel_id=1, source_target_pairs={{0,1},{1,2},{2,3},{3,4},{4,5},{5,6},{6,7},{7,8},{8,9},{9,10},{10,1... | collective-permute-start | bytes 3145736 | tf_op jit(solution)/shard_map/ppermute | solution.py:44
  147.1 5.0 %copy-start.10 = (bf16[1024,1024]{1,0:T(8,128)(2,1)S(1)}, bf16[1024,1024]{1,0:T(8,128)(2,1)}, u32[]{:S(2)}) copy-start(bf16[1024,1024]{1,0:T(8,128)(2,1)} %param.30) | copy-start | bytes 6291460
  262.9 3.9 %copy-start.11 = (bf16[1024,84]{0,1:T(8,128)(2,1)S(1)}, bf16[1024,84]{0,1:T(8,128)(2,1)}, u32[]{:S(2)}) copy-start(bf16[1024,84]{0,1:T(8,128)(2,1)} %param.33) | copy-start | bytes 516100
  262.9 3.9 %copy-start.12 = (f32[1024]{0:T(1024)S(1)}, f32[1024]{0:T(1024)}, u32[]{:S(2)}) copy-start(f32[1024]{0:T(1024)} %param.35) | copy-start | bytes 12292
  265.5 1.0 copy-start.3
  266.8 11.7 %copy-start.5 = (s32[6144,1]{0,1:T(1,128)S(1)}, s32[6144,1]{0,1:T(1,128)}, u32[]{:S(2)}) copy-start(s32[6144,1]{0,1:T(1,128)} %compare_select_fusion) | copy-start | bytes 73732
  273.9 6.2 %collective-permute-start.4 = (bf16[84,512]{1,0:T(8,128)(2,1)S(1)}, bf16[84,512]{1,0:T(8,128)(2,1)S(1)}, u32[]{:S(2)}, u32[]{:S(2)}) collective-permute-start(bf16[84,512]{1,0:T(8,128)(2,1)S(1)} %all_gather.7), channel_id=1, source_target_pairs={{0,1},{1,2},{2,3},{3,4},{4,5},{5,6},{6,7},{7,8},{8,9},{9,10},{10,1... | collective-permute-start | bytes 258056 | tf_op jit(solution)/shard_map/ppermute | solution.py:44
  278.5 6.4 %collective-permute-start.5 = (bf16[84,512]{1,0:T(8,128)(2,1)S(1)}, bf16[84,512]{1,0:T(8,128)(2,1)S(1)}, u32[]{:S(2)}, u32[]{:S(2)}) collective-permute-start(bf16[84,512]{1,0:T(8,128)(2,1)S(1)} %all_gather.7), channel_id=1, source_target_pairs={{0,63},{1,0},{2,1},{3,2},{4,3},{5,4},{6,5},{7,6},{8,7},{9,8},{10,9... | collective-permute-start | bytes 258056 | tf_op jit(solution)/shard_map/ppermute | solution.py:44
  307.7 4.2 %copy-start.2 = (bf16[84,16,128]{2,1,0:T(8,128)(2,1)S(1)}, bf16[84,16,128]{2,1,0:T(8,128)(2,1)}, u32[]{:S(2)}) copy-start(bf16[84,16,128]{2,1,0:T(8,128)(2,1)} %param.19) | copy-start | bytes 1032196
where the time goes:
time: 316 us; the launch traced here: 314 us
  matrix products  79.7 us (25%)
  other arithmetic  77.7 us (25%)
  local copies, waits for them, and re-layouts  59.2 us (19%)
  loops' own time  30.2 us (10%)
  starting transfers between devices  29.6 us (9%)
  blocking collectives  20.1 us (6%)
  waiting for transfers between devices  17.3 us (5%)
    unnamed x6, other arithmetic  48.3 us
    dot_general x16, matrix products, one_head(): jnp.dot(weights, value_head, preferred_element_type=jnp.float32)  34.6 us
    another operation x1, loops' own time, attend(): per_head = lax.map(one_head, jnp.arange(head_count, dtype=jnp.int32))  30.2 us
    ppermute x4, starting transfers between devices, passed_along(): return lax.ppermute(value, axis, pairs)  24.3 us
    dot_general x16, matrix products, one_head(): lax.dot_general(query_head, key_head, (((1,), (1,)), ((), ())), preferred...  23.4 us
    gather x1, local copies, waits for them, and re-layouts, body(): jnp.take(readout, targets.reshape(-1), axis=1)  22.1 us
    all_gather x1, blocking collectives, body(): grid_window = lax.all_gather(padded, 'lat', axis=1, tiled=True)  15.9 us
    gather x1, local copies, waits for them, and re-layouts, body(): picked = jnp.take(flat_grid, enc_src, axis=1).astype(jnp.float32)  14.9 us
  transfers between devices with their start and end apart: 7, of which 4 were waited for; matrix products, arithmetic and copies ran while one was open for 20% of the time, Pallas kernels for 0%

commit v1 on v0

v1 whole, which is shorter than its diff:
```python
import jax
import jax.numpy as jnp
from jax import lax
from jax.experimental import pallas as pl
from jax.experimental.pallas import tpu as pltpu
from jax.sharding import PartitionSpec as P

f32, bf16, i32 = jnp.float32, jnp.bfloat16, jnp.int32
MESH = pl.DeviceIdType.MESH
V = 84
D = 1024
NB = 256
KE = 16
KM = 32
ROWS = 16
COLS = 128
HALO = 16
SLOTS = 6
WINDOW = SLOTS * NB
SECTORS = 64
CHUNKS = 4
CHUNK = NB // CHUNKS
NEG = -1e30


def tile16(row):
    return jnp.broadcast_to(row, (16, row.shape[1])).astype(bf16)


def rep(tile, times):
    return jnp.concatenate([tile] * times, axis=0)


def row_codes(rows, cols, base=0):
    return (lax.broadcasted_iota(i32, (rows, cols), 0) + base).astype(f32).astype(bf16)


def flag(mask):
    return jnp.where(mask, jnp.ones((), bf16), jnp.zeros((), bf16))


def slot_of(node, lat, lon, inner):
    member = (node & (NB - 1)).astype(f32)
    device = node >> 8
    far = (device >> 6) ^ lat
    sector = device & (SECTORS - 1)
    slot = jnp.where(sector == lon, 2 * far, jnp.where(sector == inner, 1 + 2 * far, 5 - far))
    return slot.astype(f32), member


def build_enc(src, count, lat, parity, lo_ref, hi_ref, onehot_ref, a_ref):
    row = (src * 6554) >> 20
    place = src - row * (COLS + 2 * HALO)
    far = (row >> 4) ^ lat
    r = row & (ROWS - 1)
    west = place < HALO
    east = place >= HALO + COLS
    halo = west | east
    c = jnp.where(east, place - (HALO + COLS), place)
    side = jnp.where(east, 1, 0)
    outer = side ^ (1 - parity)
    hi = jnp.where(halo, 32 + 4 * far + 2 * outer + (r >> 3), 16 * far + r)
    lo = jnp.where(halo, (r & 7) * HALO + c, place - HALO)
    live = lax.broadcasted_iota(i32, src.shape, 0) < count
    hi_ref[...] = jnp.where(live, hi, -1).astype(f32)
    lo_ref[...] = lo.astype(f32)
    iota = row_codes(COLS, NB)
    for s in range(KE):
        onehot_ref[s * COLS : (s + 1) * COLS, :] = flag(iota == rep(tile16(lo_ref[s : s + 1, :]), 8))

    def group(g, carry):
        code = g.astype(f32)
        acc = jnp.zeros((COLS, NB), bf16)
        for s in range(KE):
            hit = tile16(jnp.where(hi_ref[s : s + 1, :] == code, 1.0, 0.0))
            acc = acc + onehot_ref[s * COLS : (s + 1) * COLS, :] * rep(hit, 8)
        a_ref[pl.ds(pl.multiple_of(g * COLS, COLS), COLS), :] = acc
        return carry

    lax.fori_loop(0, 40, group, 0)


def build_mask(ids, count, lat, lon, inner, hi_ref, lo_ref, hit_ref, member_ref, bias_ref):
    slot, member = slot_of(ids, lat, lon, inner)
    live = lax.broadcasted_iota(i32, ids.shape, 0) < count
    hi_ref[...] = jnp.where(live, slot, -1.0)
    lo_ref[...] = member
    for s in range(KM):
        for b in range(SLOTS):
            at = (s * SLOTS + b) * 16
            hit_ref[at : at + 16, :] = tile16(jnp.where(hi_ref[s : s + 1, :] == float(b), 1.0, 0.0))
    step = 32

    def chunk(c, carry):
        iota = row_codes(step, NB, c * step)
        acc = [jnp.zeros((step, NB), bf16) for _ in range(SLOTS)]
        for s in range(KM):
            one = flag(iota == rep(tile16(lo_ref[s : s + 1, :]), step // 16))
            for b in range(SLOTS):
                at = (s * SLOTS + b) * 16
                acc[b] = acc[b] + one * rep(hit_ref[at : at + 16, :], step // 16)
        for b in range(SLOTS):
            member_ref[b, pl.ds(pl.multiple_of(c * step, step), step), :] = acc[b]
        return carry

    lax.fori_loop(0, NB // step, chunk, 0)
    for b in range(SLOTS):
        seen = member_ref[b].astype(f32).T
        bias_ref[:, b * NB : (b + 1) * NB] = jnp.where(seen > 0.0, 0.0, NEG)


def build_dec(src_ref, lat, lon, inner, pick_ref):
    def chunk(c, carry):
        for half in range(2):
            lanes = slice(half * COLS, (half + 1) * COLS)
            codes = []
            for i in range(3):
                ids = src_ref[i, pl.ds(c * 2 + half, 1), :]
                slot, member = slot_of(ids, lat, lon, inner)
                hits = [tile16(jnp.where(slot == float(b), 1.0, 0.0)) for b in range(SLOTS)]
                codes.append((tile16(member), hits))
            for k in range(4):
                iota = row_codes(64, COLS, k * 64)
                ones = [flag(iota == rep(member, 4)) for member, _ in codes]
                for b in range(SLOTS):
                    at = b * NB + k * 64
                    pick_ref[c, at : at + 64, lanes] = (
                        ones[0] * rep(codes[0][1][b], 4)
                        + ones[1] * rep(codes[1][1][b], 4)
                        + ones[2] * rep(codes[2][1][b], 4)
                    )
        return carry

    lax.fori_loop(0, 8, chunk, 0)


def silu(u):
    return u * jax.nn.sigmoid(u)


def layer_norm(x, gain):
    centre = x - jnp.mean(x, axis=-1, keepdims=True)
    spread = jnp.mean(centre * centre, axis=-1, keepdims=True)
    return centre * lax.rsqrt(spread + 1e-05) * gain


def dot(a, b):
    return jnp.dot(a, b, preferred_element_type=f32)


def attention(q_ref, k_ref, v_ref, bias_ref, c_ref):
    low = lax.broadcasted_iota(i32, (1, 128), 1) < 64
    one, zero = jnp.ones((), bf16), jnp.zeros((), bf16)

    def pair(p, carry):
        cols = pl.ds(pl.multiple_of(p * 128, 128), 128)
        keys = k_ref[:, cols]
        values = v_ref[:, cols]
        query = q_ref[:, cols]
        outs = []
        for half in range(2):
            own = low if half == 0 else jnp.logical_not(low)
            scores = lax.dot_general(
                jnp.where(own, query, zero), keys, (((1,), (1,)), ((), ())), preferred_element_type=f32
            )
            scores = scores + bias_ref[...]
            peak = jnp.max(scores, axis=1, keepdims=True)
            expo = jnp.exp(scores - peak).astype(bf16)
            outs.append(dot(expo, jnp.where(own, values, one)))
        total = pltpu.roll(jnp.where(low, outs[1], outs[0]), 64, 1)
        c_ref[:, cols] = (jnp.where(low, outs[0], outs[1]) / total).astype(bf16)
        return carry

    lax.fori_loop(0, D // 128, pair, 0)


def kernel(
    grid_ref,
    mesh_ref,
    enc_src_ref,
    enc_count_ref,
    nbr_ref,
    nbr_count_ref,
    dec_src_ref,
    w_embed_ref,
    w_encode_hbm,
    w_query_hbm,
    w_key_hbm,
    w_value_hbm,
    w_output_hbm,
    w_decode_hbm,
    w_readout_ref,
    gain_attn_ref,
    gain_dec_ref,
    out_ref,
    halo_ref,
    mesh_w,
    mean_w,
    read_w,
    weights,
    enc_lo,
    enc_hi,
    enc_onehot,
    enc_pick,
    nbr_hi,
    nbr_lo,
    nbr_hit,
    nbr_member,
    bias_ref,
    dec_pick,
    latent_ref,
    query_ref,
    key_ref,
    value_ref,
    context_ref,
    local_sem,
    send_sem,
    recv_sem,
):
    lat = lax.axis_index("lat")
    lon = lax.axis_index("lon")
    parity = lax.rem(lon, 2)
    inner = lon + 1 - 2 * parity
    outer = lax.rem(lon + 2 * parity - 1 + SECTORS, SECTORS)
    core = (lat, inner)
    band = (1 - lat, lon)
    band_core = (1 - lat, inner)
    far = (1 - lat, outer)
    near = (lat, outer)

    loads = [
        pltpu.make_async_copy(source, weights.at[i], local_sem.at[i])
        for i, source in enumerate(
            (w_encode_hbm, w_query_hbm, w_key_hbm, w_value_hbm, w_output_hbm, w_decode_hbm)
        )
    ]
    own_load = pltpu.make_async_copy(mesh_ref, mesh_w.at[0], local_sem.at[6])

    barrier = pltpu.get_barrier_semaphore()
    for peer in (core, band, band_core, far, near):
        pl.semaphore_signal(barrier, inc=1, device_id=peer, device_id_type=MESH)
    pl.semaphore_wait(barrier, 5)

    number = iter(range(64))

    def remote(source, target, peer):
        i = next(number)
        return pltpu.make_async_remote_copy(
            src_ref=source,
            dst_ref=target,
            send_sem=send_sem.at[i],
            recv_sem=recv_sem.at[i],
            device_id=peer,
            device_id_type=MESH,
        )

    main = ROWS * COLS
    edge = ROWS * HALO
    inner_edge = pl.ds(pl.multiple_of(main + edge * (1 - parity), edge), edge)
    outer_edge = pl.ds(pl.multiple_of(main + edge * parity, edge), edge)

    def landing(i):
        return halo_ref.at[:, main + i * edge : main + (i + 1) * edge]

    grids = [
        remote(grid_ref.at[:, inner_edge], landing(0), core),
        remote(grid_ref.at[:, outer_edge], landing(1), near),
        remote(grid_ref.at[:, inner_edge], landing(2), band_core),
        remote(grid_ref.at[:, outer_edge], landing(3), far),
        remote(grid_ref.at[:, 0:main], halo_ref.at[:, 0:main], band),
    ]
    for copy in grids:
        copy.start()

    def piece(c):
        return pl.ds(c * CHUNK, CHUNK)

    to_core = remote(mesh_ref, mesh_w.at[1], core)
    to_band = [remote(mesh_ref.at[piece(c)], mesh_w.at[2, piece(c)], band) for c in range(CHUNKS)]
    to_far = [remote(mesh_ref.at[piece(c)], mesh_w.at[4, piece(c)], far) for c in range(CHUNKS)]
    on_core = [
        remote(mesh_w.at[2, piece(c)], mesh_w.at[3, piece(c)], core) for c in range(CHUNKS)
    ]
    on_near = [remote(mesh_w.at[4, piece(0)], mesh_w.at[5, piece(0)], band)] + [
        remote(mesh_w.at[2, piece(c)], mesh_w.at[5, piece(c)], far) for c in range(1, CHUNKS)
    ]
    means = [
        remote(mean_w.at[0], mean_w.at[slot], peer)
        for slot, peer in enumerate((core, band, band_core, far, near), 1)
    ]
    reads = [
        remote(read_w.at[:, 0:NB], read_w.at[:, slot * NB : (slot + 1) * NB], peer)
        for slot, peer in enumerate((core, band, band_core, far, near), 1)
    ]
    for c in range(CHUNKS):
        to_far[c].start()
        to_band[c].start()
    to_core.start()
    own_load.start()
    for load in loads:
        load.start()

    build_enc(enc_src_ref[...], enc_count_ref[...], lat, parity, enc_lo, enc_hi, enc_onehot, enc_pick)
    build_mask(
        nbr_ref[...], nbr_count_ref[...], lat, lon, inner, nbr_hi, nbr_lo, nbr_hit, nbr_member, bias_ref
    )
    for copy in grids:
        copy.wait_recv()
    summed = (
        dot(grid_ref[:, 0:main], enc_pick[0:main, :])
        + dot(halo_ref[:, 0:main], enc_pick[main : 2 * main, :])
        + dot(halo_ref[:, main:], enc_pick[2 * main :, :])
    )
    mean_w[0] = (summed / enc_count_ref[...].astype(f32)).astype(bf16)
    for copy in means:
        copy.start()

    own_load.wait()
    for load in loads:
        load.wait()

    def block(b, carry):
        @pl.when(b == 1)
        def _():
            means[0].wait_recv()
            to_core.wait_recv()
            to_far[0].wait_recv()
            on_near[0].start()
            for c in range(CHUNKS):
                to_band[c].wait_recv()
                on_core[c].start()
                if c:
                    on_near[c].start()

        @pl.when(b == 2)
        def _():
            means[1].wait_recv()

        @pl.when(b == 3)
        def _():
            means[2].wait_recv()
            for copy in on_core:
                copy.wait_recv()

        @pl.when(b == 4)
        def _():
            means[3].wait_recv()
            for copy in to_far[1:]:
                copy.wait_recv()

        @pl.when(b == 5)
        def _():
            means[4].wait_recv()
            for copy in on_near:
                copy.wait_recv()

        embedded = silu(
            lax.dot_general(
                mean_w[b], w_embed_ref[...], (((0,), (0,)), ((), ())), preferred_element_type=f32
            )
        ).astype(bf16)
        latent = mesh_w[b].astype(f32) + dot(embedded, weights[0])
        normed = layer_norm(latent, gain_attn_ref[...]).astype(bf16)
        rows = pl.ds(pl.multiple_of(b * NB, NB), NB)
        key_ref[rows, :] = dot(normed, weights[2]).astype(bf16)
        value_ref[rows, :] = dot(normed, weights[3]).astype(bf16)

        @pl.when(b == 0)
        def _():
            latent_ref[...] = latent
            query_ref[...] = (dot(normed, weights[1]).astype(bf16).astype(f32) * 0.125).astype(bf16)

        return carry

    lax.fori_loop(0, SLOTS, block, 0)

    attention(query_ref, key_ref, value_ref, bias_ref, context_ref)
    mixed = latent_ref[...] + dot(context_ref[...], weights[4])
    normed_out = layer_norm(mixed, gain_dec_ref[...]).astype(bf16)
    decoded = silu(dot(normed_out, weights[5])).astype(bf16)
    read_w[:, 0:NB] = lax.dot_general(
        w_readout_ref[...], decoded, (((0,), (1,)), ((), ())), preferred_element_type=f32
    ).astype(bf16)
    for copy in reads:
        copy.start()
    build_dec(dec_src_ref, lat, lon, inner, dec_pick)
    for copy in reads:
        copy.wait_recv()

    def finish(c, carry):
        lanes = pl.ds(pl.multiple_of(c * NB, NB), NB)
        update = dot(read_w[...], dec_pick[c])
        out_ref[:, lanes] = grid_ref[:, lanes].astype(f32) + update / 3.0
        return carry

    lax.fori_loop(0, main // NB, finish, 0)
    for copy in grids + [to_core] + to_band + to_far + on_core + on_near + means + reads:
        copy.wait_send()


def body(
    grid_state,
    mesh_feat,
    enc_src,
    enc_count,
    nbr_ids,
    nbr_count,
    dec_src,
    w_embed,
    w_encode,
    w_query,
    w_key,
    w_value,
    w_output,
    w_decode,
    w_readout,
    norm_attn,
    norm_dec,
):
    main = ROWS * COLS
    packed = jnp.concatenate(
        [
            grid_state.reshape(V, main),
            grid_state[:, :, :HALO].reshape(V, ROWS * HALO),
            grid_state[:, :, COLS - HALO :].reshape(V, ROWS * HALO),
        ],
        axis=1,
    )
    vmem = pl.BlockSpec(memory_space=pltpu.VMEM)
    hbm = pl.BlockSpec(memory_space=pl.ANY)
    out = pl.pallas_call(
        kernel,
        out_shape=jax.ShapeDtypeStruct((V, main), f32),
        in_specs=[vmem, hbm] + [vmem] * 6 + [hbm] * 6 + [vmem] * 3,
        out_specs=vmem,
        scratch_shapes=[
            pltpu.VMEM((V, main + 4 * ROWS * HALO), bf16),
            pltpu.VMEM((SLOTS, NB, D), bf16),
            pltpu.VMEM((SLOTS, V, NB), bf16),
            pltpu.VMEM((V, WINDOW), bf16),
            pltpu.VMEM((6, D, D), bf16),
            pltpu.VMEM((KE, NB), f32),
            pltpu.VMEM((KE, NB), f32),
            pltpu.VMEM((KE * COLS, NB), bf16),
            pltpu.VMEM((40 * COLS, NB), bf16),
            pltpu.VMEM((KM, NB), f32),
            pltpu.VMEM((KM, NB), f32),
            pltpu.VMEM((KM * SLOTS * 16, NB), bf16),
            pltpu.VMEM((SLOTS, NB, NB), bf16),
            pltpu.VMEM((NB, WINDOW), f32),
            pltpu.VMEM((8, WINDOW, NB), bf16),
            pltpu.VMEM((NB, D), f32),
            pltpu.VMEM((NB, D), bf16),
            pltpu.VMEM((WINDOW, D), bf16),
            pltpu.VMEM((WINDOW, D), bf16),
            pltpu.VMEM((NB, D), bf16),
            pltpu.SemaphoreType.DMA((7,)),
            pltpu.SemaphoreType.DMA((64,)),
            pltpu.SemaphoreType.DMA((64,)),
        ],
        compiler_params=pltpu.CompilerParams(
            collective_id=0, has_side_effects=True, vmem_limit_bytes=64 * 1024 * 1024 - 65536
        ),
        name="denoise",
    )(
        packed,
        mesh_feat,
        enc_src,
        enc_count.reshape(1, NB),
        nbr_ids,
        nbr_count.reshape(1, NB),
        dec_src,
        w_embed,
        w_encode,
        w_query,
        w_key,
        w_value,
        w_output,
        w_decode,
        w_readout,
        norm_attn.reshape(1, D),
        norm_dec.reshape(1, D),
    )
    return out.reshape(V, ROWS, COLS)


def solution(mesh):
    in_specs = (
        P(None, "lat", "lon"),
        P(("lat", "lon"), None),
        P(None, ("lat", "lon")),
        P(("lat", "lon")),
        P(None, ("lat", "lon")),
        P(("lat", "lon")),
        P(None, "lat", "lon"),
    ) + (P(),) * 10
    return jax.shard_map(
        body, mesh=mesh, in_specs=in_specs, out_specs=P(None, "lat", "lon"), check_vma=False
    )
```

time: 316 us -> 74 us (0.23)
  the two profiles are of different devices: /device:TPU:87 before, /device:TPU:0 now
where the time goes in v1:
time: 74 us; the launch traced here: 73.3 us
  Pallas kernels  66.2 us (89%)
  local copies, waits for them, and re-layouts  6.17 us (8%)
  other arithmetic  0.8 us (1%)
    pallas_call x1, Pallas kernels, body(): pl.pallas_call(kernel, out_shape=jax.ShapeDtypeStruct((V, main), f32), in...  66.2 us
    unnamed x6, local copies, waits for them, and re-layouts  4.17 us

profile of v1, /device:TPU:0, one launch (start us, length us, event | category | flops | bytes accessed | tf_op | source)
XLA Modules:
  0.0 73.3 jit_solution(2098599915742193279)
XLA Ops:
  0.0 0.0 copy-start
  0.0 1.8 %copy.23.w_readout_ref = bf16[1024,84]{1,0:T(8,128)(2,1)} copy(bf16[1024,84]{0,1:T(8,128)(2,1)} %param.31) | data formatting | bytes 344064 | tf_op args[14]
  1.8 1.0 %pad.3 = bf16[88,16,128]{2,1,0:T(8,128)(2,1)S(1)} pad(bf16[84,16,128]{2,1,0:T(8,128)(2,1)} %param.17, bf16[]{:T(256)} %constant.1), padding=0_4x0_0x0_0 | pad | bytes 704514
  2.8 0.1 copy.24
  2.9 0.0 copy-done
  3.0 0.2 fusion
  3.1 0.4 copy.19
  3.5 0.1 copy.21
  3.6 0.4 copy.20
  3.9 0.1 copy.22
  4.1 0.8 %pad_maximum_fusion.grid_ref = bf16[84,2560]{1,0:T(8,128)(2,1)} fusion(bf16[84,256]{1,0:T(8,128)(2,1)S(1)} %copy.22, bf16[84,256]{1,0:T(8,128)(2,1)S(1)} %copy.21, bf16[84,2048]{1,0:T(8,128)(2,1)S(1)} %bitcast.14), kind=kLoop, calls=%fused_computation | loop fusion | flops 1290240 | bytes 860160 | tf_op jit(solution)/shard_map/concatenate | solution.py:421
  4.9 66.2 %denoise.1 = f32[84,2048]{1,0:T(8,128)} custom-call(bf16[84,2560]{1,0:T(8,128)(2,1)} %pad_maximum_fusion.grid_ref, bf16[256,1024]{1,0:T(8,128)(2,1)} %mesh_ref.1, s32[16,256]{1,0:T(8,128)} %enc_src_ref.1, s32[1,256]{1,0:T(1,128)} %bitcast.20, s32[32,256]{1,0:T(8,128)} %nbr_ref.1, s32[1,256]{1,0:T(1,128)} %bitcast.21, s32[3,16,128]{2,1,0:T(8,128)} %dec_src_ref.1, ...), custom_call_target="tpu_custom_call" | custom-call | tf_op jit(solution)/shard_map/denoise/pallas_call | solution.py:431
  71.1 1.2 %copy.25 = f32[11,8,16,128]{3,2,1,0:T(8,128)S(1)} copy(f32[11,8,16,128]{3,1,2,0:T(8,128)} %bitcast.12) | data formatting | bytes 1441792
  72.4 0.9 %slice.8 = f32[84,16,128]{2,1,0:T(8,128)} slice(f32[88,16,128]{2,1,0:T(8,128)S(1)} %bitcast.13), slice={[0:84], [0:16], [0:128]} | slice | bytes 1376256 | tf_op jit(solution)/shard_map/reshape | solution.py:484
Async XLA Ops:
  0.0 2.9 %copy-start = (bf16[84,16,128]{2,1,0:T(8,128)(2,1)S(1)}, bf16[84,16,128]{2,1,0:T(8,128)(2,1)}, u32[]{:S(2)}) copy-start(bf16[84,16,128]{2,1,0:T(8,128)(2,1)} %param.17) | copy-start | bytes 1032196

commit v2 on v1

--- a/solution.py
+++ b/solution.py
@@ -20,6 +20,10 @@
 SECTORS = 64
 CHUNKS = 4
 CHUNK = NB // CHUNKS
+HEADS = 16
+HEAD = 64
+VROWS = 80
+HALF = WINDOW // 2
 NEG = -1e30
 
 
@@ -44,7 +48,7 @@
     device = node >> 8
     far = (device >> 6) ^ lat
     sector = device & (SECTORS - 1)
-    slot = jnp.where(sector == lon, 2 * far, jnp.where(sector == inner, 1 + 2 * far, 5 - far))
+    slot = jnp.where(sector == lon, 3 * far, jnp.where(sector == inner, 1 + 3 * far, 5 - 3 * far))
     return slot.astype(f32), member
 
 
@@ -80,7 +84,7 @@
     lax.fori_loop(0, 40, group, 0)
 
 
-def build_mask(ids, count, lat, lon, inner, hi_ref, lo_ref, hit_ref, member_ref, bias_ref):
+def build_mask(ids, count, lat, lon, inner, hi_ref, lo_ref, hit_ref, bias_ref):
     slot, member = slot_of(ids, lat, lon, inner)
     live = lax.broadcasted_iota(i32, ids.shape, 0) < count
     hi_ref[...] = jnp.where(live, slot, -1.0)
@@ -100,13 +104,11 @@
                 at = (s * SLOTS + b) * 16
                 acc[b] = acc[b] + one * rep(hit_ref[at : at + 16, :], step // 16)
         for b in range(SLOTS):
-            member_ref[b, pl.ds(pl.multiple_of(c * step, step), step), :] = acc[b]
+            rows = pl.ds(pl.multiple_of(b * NB + c * step, step), step)
+            bias_ref[rows, :] = jnp.where(acc[b].astype(f32) > 0.0, 0.0, NEG)
         return carry
 
     lax.fori_loop(0, NB // step, chunk, 0)
-    for b in range(SLOTS):
-        seen = member_ref[b].astype(f32).T
-        bias_ref[:, b * NB : (b + 1) * NB] = jnp.where(seen > 0.0, 0.0, NEG)
 
 
 def build_dec(src_ref, lat, lon, inner, pick_ref):
@@ -148,30 +150,45 @@
     return jnp.dot(a, b, preferred_element_type=f32)
 
 
-def attention(q_ref, k_ref, v_ref, bias_ref, c_ref):
+def attention(part, q_ref, k_ref, v_ref, bias_ref, score_refs, expo_refs, sum_ref, peak_ref, midway):
     low = lax.broadcasted_iota(i32, (1, 128), 1) < 64
-    one, zero = jnp.ones((), bf16), jnp.zeros((), bf16)
+    zero = jnp.zeros((), bf16)
+    span = pl.ds(pl.multiple_of(part * HALF, HALF), HALF)
+
+    def scores(p, half):
+        cols = pl.ds(pl.multiple_of(p * 128, 128), 128)
+        own = low if half == 0 else jnp.logical_not(low)
+        score_refs[half][...] = lax.dot_general(
+            k_ref[span, cols],
+            jnp.where(own, q_ref[:, cols], zero),
+            (((1,), (1,)), ((), ())),
+            preferred_element_type=f32,
+        )
+
+    def weigh(h, half):
+        masked = score_refs[half][...] + bias_ref[span, :]
+        peak = jnp.max(masked, axis=0, keepdims=True)
+        expo_refs[half][...] = jnp.exp(masked - peak).astype(bf16)
+        peak_ref[part, pl.ds(h, 1), :] = peak
+
+    def gather(h, half):
+        rows = pl.ds(pl.multiple_of(h * VROWS, 16), VROWS)
+        sum_ref[part, h] = dot(v_ref[rows, span], expo_refs[half][...])
+
+    scores(0, 0)
 
     def pair(p, carry):
-        cols = pl.ds(pl.multiple_of(p * 128, 128), 128)
-        keys = k_ref[:, cols]
-        values = v_ref[:, cols]
-        query = q_ref[:, cols]
-        outs = []
-        for half in range(2):
-            own = low if half == 0 else jnp.logical_not(low)
-            scores = lax.dot_general(
-                jnp.where(own, query, zero), keys, (((1,), (1,)), ((), ())), preferred_element_type=f32
-            )
-            scores = scores + bias_ref[...]
-            peak = jnp.max(scores, axis=1, keepdims=True)
-            expo = jnp.exp(scores - peak).astype(bf16)
-            outs.append(dot(expo, jnp.where(own, values, one)))
-        total = pltpu.roll(jnp.where(low, outs[1], outs[0]), 64, 1)
-        c_ref[:, cols] = (jnp.where(low, outs[0], outs[1]) / total).astype(bf16)
+        midway(p)
+        scores(p, 1)
+        gather(jnp.maximum(2 * p - 1, 0), 1)
+        weigh(2 * p, 0)
+        scores(jnp.minimum(p + 1, HEADS // 2 - 1), 0)
+        gather(2 * p, 0)
+        weigh(2 * p + 1, 1)
         return carry
 
-    lax.fori_loop(0, D // 128, pair, 0)
+    lax.fori_loop(0, HEADS // 2, pair, 0)
+    gather(HEADS - 1, 1)
 
 
 def kernel(
@@ -205,13 +222,18 @@
     nbr_hi,
     nbr_lo,
     nbr_hit,
-    nbr_member,
     bias_ref,
     dec_pick,
     latent_ref,
     query_ref,
     key_ref,
     value_ref,
+    score_a,
+    score_b,
+    expo_a,
+    expo_b,
+    sum_ref,
+    peak_ref,
     context_ref,
     local_sem,
     send_sem,
@@ -231,7 +253,7 @@
     loads = [
         pltpu.make_async_copy(source, weights.at[i], local_sem.at[i])
         for i, source in enumerate(
-            (w_encode_hbm, w_query_hbm, w_key_hbm, w_value_hbm, w_output_hbm, w_decode_hbm)
+            (w_encode_hbm, w_key_hbm, w_value_hbm, w_query_hbm, w_output_hbm, w_decode_hbm)
         )
     ]
     own_load = pltpu.make_async_copy(mesh_ref, mesh_w.at[0], local_sem.at[6])
@@ -275,35 +297,43 @@
     def piece(c):
         return pl.ds(c * CHUNK, CHUNK)
 
-    to_core = remote(mesh_ref, mesh_w.at[1], core)
-    to_band = [remote(mesh_ref.at[piece(c)], mesh_w.at[2, piece(c)], band) for c in range(CHUNKS)]
-    to_far = [remote(mesh_ref.at[piece(c)], mesh_w.at[4, piece(c)], far) for c in range(CHUNKS)]
-    on_core = [
-        remote(mesh_w.at[2, piece(c)], mesh_w.at[3, piece(c)], core) for c in range(CHUNKS)
+    to_far = [remote(mesh_ref.at[piece(c)], mesh_w.at[2, piece(c)], far) for c in (3, 0, 1, 2)]
+    to_band = [remote(mesh_ref.at[piece(c)], mesh_w.at[3, piece(c)], band) for c in range(CHUNKS)]
+    on_band = remote(mesh_w.at[2, piece(3)], mesh_w.at[5, piece(3)], band)
+    on_far = [remote(mesh_w.at[3, piece(c)], mesh_w.at[5, piece(c)], far) for c in range(3)]
+    means = [
+        remote(mean_w.at[0], mean_w.at[slot], peer) for slot, peer in ((2, far), (3, band), (5, near))
     ]
-    on_near = [remote(mesh_w.at[4, piece(0)], mesh_w.at[5, piece(0)], band)] + [
-        remote(mesh_w.at[2, piece(c)], mesh_w.at[5, piece(c)], far) for c in range(1, CHUNKS)
-    ]
-    means = [
-        remote(mean_w.at[0], mean_w.at[slot], peer)
-        for slot, peer in enumerate((core, band, band_core, far, near), 1)
+
+    def slot_rows(slot):
+        return pl.ds(slot * NB, NB)
+
+    shares = [
+        [
+            remote(key_ref.at[slot_rows(slot)], key_ref.at[slot_rows(slot + 1)], core),
+            remote(value_ref.at[:, slot_rows(slot)], value_ref.at[:, slot_rows(slot + 1)], core),
+        ]
+        for slot in (0, 3)
     ]
     reads = [
-        remote(read_w.at[:, 0:NB], read_w.at[:, slot * NB : (slot + 1) * NB], peer)
-        for slot, peer in enumerate((core, band, band_core, far, near), 1)
+        remote(read_w.at[0], read_w.at[slot], peer)
+        for slot, peer in ((1, core), (2, far), (3, band), (4, band_core), (5, near))
     ]
     for c in range(CHUNKS):
         to_far[c].start()
         to_band[c].start()
-    to_core.start()
     own_load.start()
     for load in loads:
         load.start()
 
     build_enc(enc_src_ref[...], enc_count_ref[...], lat, parity, enc_lo, enc_hi, enc_onehot, enc_pick)
-    build_mask(
-        nbr_ref[...], nbr_count_ref[...], lat, lon, inner, nbr_hi, nbr_lo, nbr_hit, nbr_member, bias_ref
-    )
+    build_mask(nbr_ref[...], nbr_count_ref[...], lat, lon, inner, nbr_hi, nbr_lo, nbr_hit, bias_ref)
+    build_dec(dec_src_ref, lat, lon, inner, dec_pick)
+    for h in range(HEADS):
+        for first, last in ((0, 1), (2, 4), (5, 6)):
+            value_ref[h * VROWS + HEAD : (h + 1) * VROWS, first * NB : last * NB] = jnp.ones(
+                (VROWS - HEAD, (last - first) * NB), bf16
+            )
     for copy in grids:
         copy.wait_recv()
     summed = (
@@ -319,82 +349,135 @@
     for load in loads:
         load.wait()
 
-    def block(b, carry):
-        @pl.when(b == 1)
+    def phase_loop(phase, carry):
+        def block(i, carry):
+            step = 2 * phase + i
+
+            @pl.when(step == 1)
+            def _():
+                to_far[0].wait_recv()
+                on_band.start()
+                to_band[0].wait_recv()
+                on_far[0].start()
+                means[0].wait_recv()
+                for copy in to_far[1:]:
+                    copy.wait_recv()
+                for copy in shares[0]:
+                    copy.start()
+
+            @pl.when(step == 2)
+            def _():
+                means[1].wait_recv()
+                to_band[3].wait_recv()
+
+            @pl.when(step == 3)
+            def _():
+                means[2].wait_recv()
+                on_band.wait_recv()
+                for copy in on_far:
+                    copy.wait_recv()
+                for copy in shares[1]:
+                    copy.start()
+
+            slot = 3 * phase + 2 * i
+            embedded = silu(
+                lax.dot_general(
+                    mean_w[slot], w_embed_ref[...], (((0,), (0,)), ((), ())), preferred_element_type=f32
+                )
+            ).astype(bf16)
+            latent = mesh_w[slot].astype(f32) + dot(embedded, weights[0])
+            normed = layer_norm(latent, gain_attn_ref[...]).astype(bf16)
+            rows = pl.ds(pl.multiple_of(slot * NB, NB), NB)
+            key_ref[rows, :] = dot(normed, weights[1]).astype(bf16)
+            values = dot(normed, weights[2]).T.astype(bf16)
+            for h in range(HEADS):
+                value_ref[h * VROWS : h * VROWS + HEAD, rows] = values[h * HEAD : (h + 1) * HEAD, :]
+
+            @pl.when(step == 0)
+            def _():
+                latent_ref[...] = latent
+                query_ref[...] = (dot(normed, weights[3]).astype(bf16).astype(f32) * 0.125).astype(bf16)
+
+            return carry
+
+        lax.fori_loop(0, 2, block, 0)
+
+        @pl.when(phase == 0)
         def _():
-            means[0].wait_recv()
-            to_core.wait_recv()
-            to_far[0].wait_recv()
-            on_near[0].start()
-            for c in range(CHUNKS):
-                to_band[c].wait_recv()
-                on_core[c].start()
-                if c:
-                    on_near[c].start()
-
-        @pl.when(b == 2)
+            to_band[1].wait_recv()
+            on_far[1].start()
+            for copy in shares[0]:
+                copy.wait_recv()
+
+        @pl.when(phase == 1)
         def _():
-            means[1].wait_recv()
-
-        @pl.when(b == 3)
-        def _():
-            means[2].wait_recv()
-            for copy in on_core:
+            for copy in shares[1]:
                 copy.wait_recv()
 
-        @pl.when(b == 4)
-        def _():
-            means[3].wait_recv()
-            for copy in to_far[1:]:
-                copy.wait_recv()
-
-        @pl.when(b == 5)
-        def _():
-            means[4].wait_recv()
-            for copy in on_near:
-                copy.wait_recv()
-
-        embedded = silu(
-            lax.dot_general(
-                mean_w[b], w_embed_ref[...], (((0,), (0,)), ((), ())), preferred_element_type=f32
-            )
+        def midway(p):
+            @pl.when(jnp.logical_and(phase == 0, p == HEADS // 4))
+            def _():
+                to_band[2].wait_recv()
+                on_far[2].start()
+
+        attention(
+            phase,
+            query_ref,
+            key_ref,
+            value_ref,
+            bias_ref,
+            (score_a, score_b),
+            (expo_a, expo_b),
+            sum_ref,
+            peak_ref,
+            midway,
+        )
+        return carry
+
+    lax.fori_loop(0, 2, phase_loop, 0)
+
+    def merge(h, carry):
+        peak_a = peak_ref[0, pl.ds(h, 1), :]
+        peak_b = peak_ref[1, pl.ds(h, 1), :]
+        peak = jnp.maximum(peak_a, peak_b)
+        joined = sum_ref[0, h] * jnp.exp(peak_a - peak) + sum_ref[1, h] * jnp.exp(peak_b - peak)
+        context_ref[pl.ds(pl.multiple_of(h * HEAD, HEAD), HEAD), :] = (
+            joined[0:HEAD, :] / joined[HEAD : HEAD + 1, :]
         ).astype(bf16)
-        latent = mesh_w[b].astype(f32) + dot(embedded, weights[0])
-        normed = layer_norm(latent, gain_attn_ref[...]).astype(bf16)
-        rows = pl.ds(pl.multiple_of(b * NB, NB), NB)
-        key_ref[rows, :] = dot(normed, weights[2]).astype(bf16)
-        value_ref[rows, :] = dot(normed, weights[3]).astype(bf16)
-
-        @pl.when(b == 0)
-        def _():
-            latent_ref[...] = latent
-            query_ref[...] = (dot(normed, weights[1]).astype(bf16).astype(f32) * 0.125).astype(bf16)
-
         return carry
 
-    lax.fori_loop(0, SLOTS, block, 0)
-
-    attention(query_ref, key_ref, value_ref, bias_ref, context_ref)
-    mixed = latent_ref[...] + dot(context_ref[...], weights[4])
+    lax.fori_loop(0, HEADS, merge, 0)
+    mixed = latent_ref[...] + lax.dot_general(
+        context_ref[...], weights[4], (((0,), (0,)), ((), ())), preferred_element_type=f32
+    )
     normed_out = layer_norm(mixed, gain_dec_ref[...]).astype(bf16)
     decoded = silu(dot(normed_out, weights[5])).astype(bf16)
-    read_w[:, 0:NB] = lax.dot_general(
-        w_readout_ref[...], decoded, (((0,), (1,)), ((), ())), preferred_element_type=f32
+    read_w[0] = lax.dot_general(
+        w_readout_ref[...], decoded, (((1,), (1,)), ((), ())), preferred_element_type=f32
     ).astype(bf16)
     for copy in reads:
         copy.start()
-    build_dec(dec_src_ref, lat, lon, inner, dec_pick)
-    for copy in reads:
+
+    def add_slots(slots, first, last):
+        def chunk(c, carry):
+            lanes = pl.ds(pl.multiple_of(c * NB, NB), NB)
+            update = sum(dot(read_w[b], dec_pick[c, b * NB : (b + 1) * NB, :]) for b in slots)
+            if not first:
+                update = update + out_ref[:, lanes]
+            if last:
+                update = grid_ref[:, lanes].astype(f32) + update / 3.0
+            out_ref[:, lanes] = update
+            return carry
+
+        lax.fori_loop(0, main // NB, chunk, 0)
+
+    add_slots((0,), True, False)
+    reads[0].wait_recv()
+    add_slots((1,), False, False)
+    for copy in reads[1:]:
         copy.wait_recv()
-
-    def finish(c, carry):
-        lanes = pl.ds(pl.multiple_of(c * NB, NB), NB)
-        update = dot(read_w[...], dec_pick[c])
-        out_ref[:, lanes] = grid_ref[:, lanes].astype(f32) + update / 3.0
-        return carry
-
-    lax.fori_loop(0, main // NB, finish, 0)
-    for copy in grids + [to_core] + to_band + to_far + on_core + on_near + means + reads:
+    add_slots((2, 3, 4, 5), False, True)
+    for copy in grids + to_far + to_band + [on_band] + on_far + means + shares[0] + shares[1] + reads:
         copy.wait_send()
 
 
@@ -437,7 +520,7 @@
             pltpu.VMEM((V, main + 4 * ROWS * HALO), bf16),
             pltpu.VMEM((SLOTS, NB, D), bf16),
             pltpu.VMEM((SLOTS, V, NB), bf16),
-            pltpu.VMEM((V, WINDOW), bf16),
+            pltpu.VMEM((SLOTS, V, NB), bf16),
             pltpu.VMEM((6, D, D), bf16),
             pltpu.VMEM((KE, NB), f32),
             pltpu.VMEM((KE, NB), f32),
@@ -446,14 +529,19 @@
             pltpu.VMEM((KM, NB), f32),
             pltpu.VMEM((KM, NB), f32),
             pltpu.VMEM((KM * SLOTS * 16, NB), bf16),
-            pltpu.VMEM((SLOTS, NB, NB), bf16),
-            pltpu.VMEM((NB, WINDOW), f32),
+            pltpu.VMEM((WINDOW, NB), f32),
             pltpu.VMEM((8, WINDOW, NB), bf16),
             pltpu.VMEM((NB, D), f32),
             pltpu.VMEM((NB, D), bf16),
             pltpu.VMEM((WINDOW, D), bf16),
-            pltpu.VMEM((WINDOW, D), bf16),
-            pltpu.VMEM((NB, D), bf16),
+            pltpu.VMEM((HEADS * VROWS, WINDOW), bf16),
+            pltpu.VMEM((HALF, NB), f32),
+            pltpu.VMEM((HALF, NB), f32),
+            pltpu.VMEM((HALF, NB), bf16),
+            pltpu.VMEM((HALF, NB), bf16),
+            pltpu.VMEM((2, HEADS, VROWS, NB), f32),
+            pltpu.VMEM((2, HEADS, NB), f32),
+            pltpu.VMEM((D, NB), bf16),
             pltpu.SemaphoreType.DMA((7,)),
             pltpu.SemaphoreType.DMA((64,)),
             pltpu.SemaphoreType.DMA((64,)),
@@ -477,7 +565,7 @@
         w_value,
         w_output,
         w_decode,
-        w_readout,
+        w_readout.T,
         norm_attn.reshape(1, D),
         norm_dec.reshape(1, D),
     )

time: 74 us -> 63.1 us (0.85)
  Pallas kernels: 66.2 us -> 56.6 us
  local copies, waits for them, and re-layouts: 6.17 us -> 5.43 us
    pallas_call x1, Pallas kernels: 66.2 us -> 56.6 us  [body(): pl.pallas_call(kernel, out_shape=jax.ShapeDtypeStruct((V, main), f32), in...]
    unnamed x6 -> x3, local copies, waits for them, and re-layouts: 4.17 us -> 2.34 us
    slice x2, local copies, waits for them, and re-layouts: 0.52 us -> 1.6 us  [body(): grid_state[:, :, :HALO].reshape(V, ROWS * HALO)]
where the time goes in v2:
time: 63.1 us; the launch traced here: 62.9 us
  Pallas kernels  56.6 us (90%)
  local copies, waits for them, and re-layouts  5.43 us (9%)
  other arithmetic  0.8 us (1%)
    pallas_call x1, Pallas kernels, body(): pl.pallas_call(kernel, out_shape=jax.ShapeDtypeStruct((V, main), f32), in...  56.6 us
    unnamed x3, local copies, waits for them, and re-layouts  2.34 us
    slice x2, local copies, waits for them, and re-layouts, body(): grid_state[:, :, :HALO].reshape(V, ROWS * HALO)  1.6 us

profile of v2, /device:TPU:0, one launch (start us, length us, event | category | flops | bytes accessed | tf_op | source)
XLA Modules:
  0.0 62.9 jit_solution(11723982330679286140)
XLA Ops:
  0.0 1.0 %pad.3 = bf16[88,16,128]{2,1,0:T(8,128)(2,1)S(1)} pad(bf16[84,16,128]{2,1,0:T(8,128)(2,1)} %param.17, bf16[]{:T(256)} %constant.1), padding=0_4x0_0x0_0 | pad | bytes 704514
  1.0 0.1 copy.22
  1.1 1.2 %fusion = (bf16[84,16,16]{2,1,0:T(8,128)(2,1)S(1)}, bf16[84,16,16]{2,1,0:T(8,128)(2,1)S(1)}) fusion(bf16[84,16,128]{2,1,0:T(8,128)(2,1)} %param.17), kind=kLoop, calls=%fused_computation.1 | loop fusion | bytes 172032 | tf_op jit(solution)/shard_map/slice | solution.py:507
  2.4 0.4 copy.18
  2.7 0.1 copy.20
  2.8 0.4 copy.19
  3.2 0.1 copy.21
  3.3 0.8 %pad_maximum_fusion.grid_ref = bf16[84,2560]{1,0:T(8,128)(2,1)} fusion(bf16[84,256]{1,0:T(8,128)(2,1)S(1)} %copy.21, bf16[84,256]{1,0:T(8,128)(2,1)S(1)} %copy.20, bf16[84,2048]{1,0:T(8,128)(2,1)S(1)} %bitcast.15), kind=kLoop, calls=%fused_computation | loop fusion | flops 1290240 | bytes 860160 | tf_op jit(solution)/shard_map/concatenate | solution.py:504
  4.1 56.6 %denoise.1 = f32[84,2048]{1,0:T(8,128)} custom-call(bf16[84,2560]{1,0:T(8,128)(2,1)} %pad_maximum_fusion.grid_ref, bf16[256,1024]{1,0:T(8,128)(2,1)} %mesh_ref.1, s32[16,256]{1,0:T(8,128)} %enc_src_ref.1, s32[1,256]{1,0:T(1,128)} %bitcast.22, s32[32,256]{1,0:T(8,128)} %nbr_ref.1, s32[1,256]{1,0:T(1,128)} %bitcast.23, s32[3,16,128]{2,1,0:T(8,128)} %dec_src_ref.1, ...), custom_call_target="tpu_custom_call" | custom-call | tf_op jit(solution)/shard_map/denoise/pallas_call | solution.py:514
  60.7 1.2 %copy.23 = f32[11,8,16,128]{3,2,1,0:T(8,128)S(1)} copy(f32[11,8,16,128]{3,1,2,0:T(8,128)} %bitcast.13) | data formatting | bytes 1441792
  62.0 0.9 %slice.8 = f32[84,16,128]{2,1,0:T(8,128)} slice(f32[88,16,128]{2,1,0:T(8,128)S(1)} %bitcast.14), slice={[0:84], [0:16], [0:128]} | slice | bytes 1376256 | tf_op jit(solution)/shard_map/reshape | solution.py:572

commit v3 on v2

--- a/solution.py
+++ b/solution.py
@@ -52,10 +52,26 @@
     return slot.astype(f32), member
 
 
+def pack_grid(grid_ref, flat_ref, edge_ref):
+    rows = jnp.transpose(grid_ref[...], (1, 0, 2))
+    lane = lax.broadcasted_iota(i32, (1, COLS), 1)
+    for r in range(ROWS):
+        flat_ref[:, r * COLS : (r + 1) * COLS] = rows[r]
+    for east in range(2):
+        for half in range(2):
+            strip = jnp.zeros((V, COLS), f32)
+            for k in range(8):
+                row = rows[half * 8 + k].astype(f32)
+                turn = (k * HALO - (COLS - HALO) * east) % COLS
+                row = pltpu.roll(row, turn, 1) if turn else row
+                strip = jnp.where((lane >= k * HALO) & (lane < (k + 1) * HALO), row, strip)
+            at = (2 * east + half) * COLS
+            edge_ref[:, at : at + COLS] = strip.astype(bf16)
+
+
 def build_enc(src, count, lat, parity, lo_ref, hi_ref, onehot_ref, a_ref):
     row = (src * 6554) >> 20
     place = src - row * (COLS + 2 * HALO)
-    far = (row >> 4) ^ lat
     r = row & (ROWS - 1)
     west = place < HALO
     east = place >= HALO + COLS
@@ -63,9 +79,9 @@
     c = jnp.where(east, place - (HALO + COLS), place)
     side = jnp.where(east, 1, 0)
     outer = side ^ (1 - parity)
-    hi = jnp.where(halo, 32 + 4 * far + 2 * outer + (r >> 3), 16 * far + r)
+    hi = jnp.where(halo, 16 + 2 * outer + (r >> 3), r)
     lo = jnp.where(halo, (r & 7) * HALO + c, place - HALO)
-    live = lax.broadcasted_iota(i32, src.shape, 0) < count
+    live = (lax.broadcasted_iota(i32, src.shape, 0) < count) & ((row >> 4) == lat)
     hi_ref[...] = jnp.where(live, hi, -1).astype(f32)
     lo_ref[...] = lo.astype(f32)
     iota = row_codes(COLS, NB)
@@ -81,7 +97,7 @@
         a_ref[pl.ds(pl.multiple_of(g * COLS, COLS), COLS), :] = acc
         return carry
 
-    lax.fori_loop(0, 40, group, 0)
+    lax.fori_loop(0, 20, group, 0)
 
 
 def build_mask(ids, count, lat, lon, inner, hi_ref, lo_ref, hit_ref, bias_ref):
@@ -150,7 +166,7 @@
     return jnp.dot(a, b, preferred_element_type=f32)
 
 
-def attention(part, q_ref, k_ref, v_ref, bias_ref, score_refs, expo_refs, sum_ref, peak_ref, midway):
+def attention(part, q_ref, k_ref, v_ref, bias_ref, score_refs, expo_refs, sum_ref, peak_ref):
     low = lax.broadcasted_iota(i32, (1, 128), 1) < 64
     zero = jnp.zeros((), bf16)
     span = pl.ds(pl.multiple_of(part * HALF, HALF), HALF)
@@ -178,7 +194,6 @@
     scores(0, 0)
 
     def pair(p, carry):
-        midway(p)
         scores(p, 1)
         gather(jnp.maximum(2 * p - 1, 0), 1)
         weigh(2 * p, 0)
@@ -210,7 +225,14 @@
     gain_attn_ref,
     gain_dec_ref,
     out_ref,
+    flat_ref,
+    edge_ref,
     halo_ref,
+    peer_src,
+    peer_count,
+    part_out,
+    part_in,
+    total_ref,
     mesh_w,
     mean_w,
     read_w,
@@ -219,6 +241,7 @@
     enc_hi,
     enc_onehot,
     enc_pick,
+    peer_pick,
     nbr_hi,
     nbr_lo,
     nbr_hit,
@@ -261,6 +284,10 @@
     barrier = pltpu.get_barrier_semaphore()
     for peer in (core, band, band_core, far, near):
         pl.semaphore_signal(barrier, inc=1, device_id=peer, device_id_type=MESH)
+    own_load.start()
+    for load in loads:
+        load.start()
+    pack_grid(grid_ref, flat_ref, edge_ref)
     pl.semaphore_wait(barrier, 5)
 
     number = iter(range(64))
@@ -278,29 +305,26 @@
 
     main = ROWS * COLS
     edge = ROWS * HALO
-    inner_edge = pl.ds(pl.multiple_of(main + edge * (1 - parity), edge), edge)
-    outer_edge = pl.ds(pl.multiple_of(main + edge * parity, edge), edge)
-
-    def landing(i):
-        return halo_ref.at[:, main + i * edge : main + (i + 1) * edge]
-
+    inner_edge = pl.ds(pl.multiple_of(edge * (1 - parity), edge), edge)
+    outer_edge = pl.ds(pl.multiple_of(edge * parity, edge), edge)
     grids = [
-        remote(grid_ref.at[:, inner_edge], landing(0), core),
-        remote(grid_ref.at[:, outer_edge], landing(1), near),
-        remote(grid_ref.at[:, inner_edge], landing(2), band_core),
-        remote(grid_ref.at[:, outer_edge], landing(3), far),
-        remote(grid_ref.at[:, 0:main], halo_ref.at[:, 0:main], band),
+        remote(enc_src_ref, peer_src, band),
+        remote(enc_count_ref, peer_count, band),
+        remote(edge_ref.at[:, inner_edge], halo_ref.at[:, 0:edge], core),
+        remote(edge_ref.at[:, outer_edge], halo_ref.at[:, edge : 2 * edge], near),
     ]
+    part = remote(part_out, part_in, band)
     for copy in grids:
         copy.start()
 
     def piece(c):
         return pl.ds(c * CHUNK, CHUNK)
 
-    to_far = [remote(mesh_ref.at[piece(c)], mesh_w.at[2, piece(c)], far) for c in (3, 0, 1, 2)]
+    order = (2, 3, 0, 1)
+    to_far = {c: remote(mesh_ref.at[piece(c)], mesh_w.at[2, piece(c)], far) for c in order}
     to_band = [remote(mesh_ref.at[piece(c)], mesh_w.at[3, piece(c)], band) for c in range(CHUNKS)]
-    on_band = remote(mesh_w.at[2, piece(3)], mesh_w.at[5, piece(3)], band)
-    on_far = [remote(mesh_w.at[3, piece(c)], mesh_w.at[5, piece(c)], far) for c in range(3)]
+    on_band = {c: remote(mesh_w.at[2, piece(c)], mesh_w.at[5, piece(c)], band) for c in (2, 3)}
+    on_far = [remote(mesh_w.at[3, piece(c)], mesh_w.at[5, piece(c)], far) for c in range(2)]
     means = [
         remote(mean_w.at[0], mean_w.at[slot], peer) for slot, peer in ((2, far), (3, band), (5, near))
     ]
@@ -319,34 +343,39 @@
         remote(read_w.at[0], read_w.at[slot], peer)
         for slot, peer in ((1, core), (2, far), (3, band), (4, band_core), (5, near))
     ]
-    for c in range(CHUNKS):
+    for c in order:
         to_far[c].start()
+    to_band[0].start()
+
+    build_enc(enc_src_ref[...], enc_count_ref[...], lat, parity, enc_lo, enc_hi, enc_onehot, enc_pick)
+    for copy in grids[:2]:
+        copy.wait_recv()
+    build_enc(peer_src[...], peer_count[...], lat, parity, enc_lo, enc_hi, enc_onehot, peer_pick)
+    for copy in grids[2:]:
+        copy.wait_recv()
+    part_out[...] = dot(flat_ref[...], peer_pick[0:main, :]) + dot(halo_ref[...], peer_pick[main:, :])
+    summed = dot(flat_ref[...], enc_pick[0:main, :]) + dot(halo_ref[...], enc_pick[main:, :])
+    part.start()
+    for c in range(1, CHUNKS):
         to_band[c].start()
-    own_load.start()
-    for load in loads:
-        load.start()
-
-    build_enc(enc_src_ref[...], enc_count_ref[...], lat, parity, enc_lo, enc_hi, enc_onehot, enc_pick)
-    build_mask(nbr_ref[...], nbr_count_ref[...], lat, lon, inner, nbr_hi, nbr_lo, nbr_hit, bias_ref)
-    build_dec(dec_src_ref, lat, lon, inner, dec_pick)
+    to_far[2].wait_recv()
+    on_band[2].start()
+    to_band[0].wait_recv()
+    on_far[0].start()
     for h in range(HEADS):
         for first, last in ((0, 1), (2, 4), (5, 6)):
             value_ref[h * VROWS + HEAD : (h + 1) * VROWS, first * NB : last * NB] = jnp.ones(
                 (VROWS - HEAD, (last - first) * NB), bf16
             )
-    for copy in grids:
-        copy.wait_recv()
-    summed = (
-        dot(grid_ref[:, 0:main], enc_pick[0:main, :])
-        + dot(halo_ref[:, 0:main], enc_pick[main : 2 * main, :])
-        + dot(halo_ref[:, main:], enc_pick[2 * main :, :])
-    )
-    mean_w[0] = (summed / enc_count_ref[...].astype(f32)).astype(bf16)
+    build_dec(dec_src_ref, lat, lon, inner, dec_pick)
+    part.wait_recv()
+    mean_w[0] = ((summed + part_in[...]) / enc_count_ref[...].astype(f32)).astype(bf16)
+    to_far[3].wait_recv()
+    on_band[3].start()
+    own_load.wait()
     for copy in means:
         copy.start()
-
-    own_load.wait()
-    for load in loads:
+    for load in loads[:4]:
         load.wait()
 
     def phase_loop(phase, carry):
@@ -355,29 +384,28 @@
 
             @pl.when(step == 1)
             def _():
-                to_far[0].wait_recv()
-                on_band.start()
-                to_band[0].wait_recv()
-                on_far[0].start()
-                means[0].wait_recv()
-                for copy in to_far[1:]:
-                    copy.wait_recv()
+                to_band[1].wait_recv()
+                on_far[1].start()
                 for copy in shares[0]:
                     copy.start()
+                build_mask(nbr_ref[...], nbr_count_ref[...], lat, lon, inner, nbr_hi, nbr_lo, nbr_hit, bias_ref)
+                to_far[0].wait_recv()
+                to_far[1].wait_recv()
+                means[0].wait_recv()
 
             @pl.when(step == 2)
             def _():
                 means[1].wait_recv()
+                to_band[2].wait_recv()
                 to_band[3].wait_recv()
 
             @pl.when(step == 3)
             def _():
-                means[2].wait_recv()
-                on_band.wait_recv()
-                for copy in on_far:
-                    copy.wait_recv()
                 for copy in shares[1]:
                     copy.start()
+                means[2].wait_recv()
+                for copy in (on_band[2], on_band[3], on_far[0], on_far[1]):
+                    copy.wait_recv()
 
             slot = 3 * phase + 2 * i
             embedded = silu(
@@ -404,8 +432,6 @@
 
         @pl.when(phase == 0)
         def _():
-            to_band[1].wait_recv()
-            on_far[1].start()
             for copy in shares[0]:
                 copy.wait_recv()
 
@@ -413,12 +439,6 @@
         def _():
             for copy in shares[1]:
                 copy.wait_recv()
-
-        def midway(p):
-            @pl.when(jnp.logical_and(phase == 0, p == HEADS // 4))
-            def _():
-                to_band[2].wait_recv()
-                on_far[2].start()
 
         attention(
             phase,
@@ -430,7 +450,6 @@
             (expo_a, expo_b),
             sum_ref,
             peak_ref,
-            midway,
         )
         return carry
 
@@ -447,6 +466,8 @@
         return carry
 
     lax.fori_loop(0, HEADS, merge, 0)
+    for load in loads[4:]:
+        load.wait()
     mixed = latent_ref[...] + lax.dot_general(
         context_ref[...], weights[4], (((0,), (0,)), ((), ())), preferred_element_type=f32
     )
@@ -463,10 +484,13 @@
             lanes = pl.ds(pl.multiple_of(c * NB, NB), NB)
             update = sum(dot(read_w[b], dec_pick[c, b * NB : (b + 1) * NB, :]) for b in slots)
             if not first:
-                update = update + out_ref[:, lanes]
+                update = update + total_ref[:, lanes]
             if last:
-                update = grid_ref[:, lanes].astype(f32) + update / 3.0
-            out_ref[:, lanes] = update
+                update = flat_ref[:, lanes].astype(f32) + update / 3.0
+                out_ref[:, 2 * c, :] = update[:, :COLS]
+                out_ref[:, 2 * c + 1, :] = update[:, COLS:]
+            else:
+                total_ref[:, lanes] = update
             return carry
 
         lax.fori_loop(0, main // NB, chunk, 0)
@@ -477,7 +501,8 @@
     for copy in reads[1:]:
         copy.wait_recv()
     add_slots((2, 3, 4, 5), False, True)
-    for copy in grids + to_far + to_band + [on_band] + on_far + means + shares[0] + shares[1] + reads:
+    blocks = list(to_far.values()) + to_band + list(on_band.values()) + on_far
+    for copy in grids + [part] + blocks + means + shares[0] + shares[1] + reads:
         copy.wait_send()
 
 
@@ -501,23 +526,22 @@
     norm_dec,
 ):
     main = ROWS * COLS
-    packed = jnp.concatenate(
-        [
-            grid_state.reshape(V, main),
-            grid_state[:, :, :HALO].reshape(V, ROWS * HALO),
-            grid_state[:, :, COLS - HALO :].reshape(V, ROWS * HALO),
-        ],
-        axis=1,
-    )
     vmem = pl.BlockSpec(memory_space=pltpu.VMEM)
     hbm = pl.BlockSpec(memory_space=pl.ANY)
     out = pl.pallas_call(
         kernel,
-        out_shape=jax.ShapeDtypeStruct((V, main), f32),
+        out_shape=jax.ShapeDtypeStruct((V, ROWS, COLS), f32),
         in_specs=[vmem, hbm] + [vmem] * 6 + [hbm] * 6 + [vmem] * 3,
         out_specs=vmem,
         scratch_shapes=[
-            pltpu.VMEM((V, main + 4 * ROWS * HALO), bf16),
+            pltpu.VMEM((V, main), bf16),
+            pltpu.VMEM((V, 2 * ROWS * HALO), bf16),
+            pltpu.VMEM((V, 2 * ROWS * HALO), bf16),
+            pltpu.VMEM((KE, NB), i32),
+            pltpu.VMEM((1, NB), i32),
+            pltpu.VMEM((V, NB), f32),
+            pltpu.VMEM((V, NB), f32),
+            pltpu.VMEM((V, main), f32),
             pltpu.VMEM((SLOTS, NB, D), bf16),
             pltpu.VMEM((SLOTS, V, NB), bf16),
             pltpu.VMEM((SLOTS, V, NB), bf16),
@@ -525,7 +549,8 @@
             pltpu.VMEM((KE, NB), f32),
             pltpu.VMEM((KE, NB), f32),
             pltpu.VMEM((KE * COLS, NB), bf16),
-            pltpu.VMEM((40 * COLS, NB), bf16),
+            pltpu.VMEM((20 * COLS, NB), bf16),
+            pltpu.VMEM((20 * COLS, NB), bf16),
             pltpu.VMEM((KM, NB), f32),
             pltpu.VMEM((KM, NB), f32),
             pltpu.VMEM((KM * SLOTS * 16, NB), bf16),
@@ -551,7 +576,7 @@
         ),
         name="denoise",
     )(
-        packed,
+        grid_state,
         mesh_feat,
         enc_src,
         enc_count.reshape(1, NB),
@@ -569,7 +594,7 @@
         norm_attn.reshape(1, D),
         norm_dec.reshape(1, D),
     )
-    return out.reshape(V, ROWS, COLS)
+    return out
 
 
 def solution(mesh):

time: 63.1 us -> 58.9 us (0.933)
  local copies, waits for them, and re-layouts: 5.43 us -> 1.99 us
  other arithmetic: 0.8 us -> 0 us
    slice x3 -> x0, local copies, waits for them, and re-layouts: 1.96 us -> none  [the longest x2 1.6 us: body(): grid_state[:, :, :HALO].reshape(V, ROWS * HALO)]
    reshape x3 -> x0, local copies, waits for them, and re-layouts: 1.12 us -> none  [the longest x1 0.89 us: body(): return out.reshape(V, ROWS, COLS)]
    concatenate x1 -> x0, other arithmetic: 0.8 us -> none  [body(): jnp.concatenate([grid_state.reshape(V, main), grid_state[:, :, :HALO].res...]
    unnamed x3 -> x1, local copies, waits for them, and re-layouts: 2.34 us -> 1.99 us
where the time goes in v3:
time: 58.9 us; the launch traced here: 58.8 us
  Pallas kernels  56.8 us (96%)
  local copies, waits for them, and re-layouts  1.99 us (3%)
    pallas_call x1, Pallas kernels, body(): pl.pallas_call(kernel, out_shape=jax.ShapeDtypeStruct((V, ROWS, COLS), f3...  56.8 us
    unnamed x1, local copies, waits for them, and re-layouts  1.99 us

profile of v3, /device:TPU:0, one launch (start us, length us, event | category | flops | bytes accessed | tf_op | source)
XLA Modules:
  0.0 58.8 jit_solution(2008359334755691279)
XLA Ops:
  0.0 56.8 %denoise.1 = f32[84,16,128]{2,1,0:T(8,128)} custom-call(bf16[84,16,128]{2,1,0:T(8,128)(2,1)} %grid_ref.1, bf16[256,1024]{1,0:T(8,128)(2,1)} %mesh_ref.1, s32[16,256]{1,0:T(8,128)} %enc_src_ref.1, s32[1,256]{1,0:T(1,128)} %bitcast.8, s32[32,256]{1,0:T(8,128)} %nbr_ref.1, s32[1,256]{1,0:T(1,128)} %bitcast.9, s32[3,16,128]{2,1,0:T(8,128)} %dec_src_ref.1, ...), custom_call_target="tpu_custom_call" | custom-call | tf_op jit(solution)/shard_map/denoise/pallas_call | solution.py:531
  56.8 2.0 %copy.19 = f32[84,16,128]{2,1,0:T(8,128)} copy(f32[84,16,128]{2,1,0:T(8,128)} %denoise.1) | data formatting | bytes 1376256

commit v4 on v3

--- a/solution.py
+++ b/solution.py
@@ -23,6 +23,7 @@
 HEADS = 16
 HEAD = 64
 VROWS = 80
+HB = NB // 2
 HALF = WINDOW // 2
 NEG = -1e30
 
@@ -120,7 +121,9 @@
                 at = (s * SLOTS + b) * 16
                 acc[b] = acc[b] + one * rep(hit_ref[at : at + 16, :], step // 16)
         for b in range(SLOTS):
-            rows = pl.ds(pl.multiple_of(b * NB + c * step, step), step)
+            shift = jnp.where(c < NB // step // 2, 0, HB)
+            start = (0, NB, 2 * NB + shift, 3 * NB + HB - 3 * shift, 4 * NB, 5 * NB)[b]
+            rows = pl.ds(pl.multiple_of(start + c * step, step), step)
             bias_ref[rows, :] = jnp.where(acc[b].astype(f32) > 0.0, 0.0, NEG)
         return carry
 
@@ -320,61 +323,74 @@
     def piece(c):
         return pl.ds(c * CHUNK, CHUNK)
 
+    def place(unit, half, c):
+        return mesh_w.at[unit, pl.ds(half * HB + c % 2 * CHUNK, CHUNK)]
+
     order = (2, 3, 0, 1)
-    to_far = {c: remote(mesh_ref.at[piece(c)], mesh_w.at[2, piece(c)], far) for c in order}
-    to_band = [remote(mesh_ref.at[piece(c)], mesh_w.at[3, piece(c)], band) for c in range(CHUNKS)]
-    on_band = {c: remote(mesh_w.at[2, piece(c)], mesh_w.at[5, piece(c)], band) for c in (2, 3)}
-    on_far = [remote(mesh_w.at[3, piece(c)], mesh_w.at[5, piece(c)], far) for c in range(2)]
+    to_far = [remote(mesh_ref.at[piece(c)], place(1 + c // 2, 0, c), far) for c in range(CHUNKS)]
+    to_band = {c: remote(mesh_ref.at[piece(c)], place(2 - c // 2, 1, c), band) for c in order}
+    on_band = [remote(place(1, 0, c), place(3, 0, c), band) for c in (0, 1)]
+    on_far = [remote(place(1, 1, c), place(3, 1, c), far) for c in (2, 3)]
     means = [
-        remote(mean_w.at[0], mean_w.at[slot], peer) for slot, peer in ((2, far), (3, band), (5, near))
+        remote(mean_w.at[0], mean_w.at[2], far),
+        remote(mean_w.at[1], mean_w.at[3], band),
+        remote(mean_w.at[1], mean_w.at[4], far),
+        remote(mean_w.at[0], mean_w.at[5], band),
+        remote(mean_w.at[0:2], mean_w.at[6:8], near),
     ]
 
-    def slot_rows(slot):
-        return pl.ds(slot * NB, NB)
+    def share(start, size, target):
+        source, target = pl.ds(start, size), pl.ds(target, size)
+        return [
+            remote(key_ref.at[source], key_ref.at[target], core),
+            remote(value_ref.at[:, source], value_ref.at[:, target], core),
+        ]
 
     shares = [
-        [
-            remote(key_ref.at[slot_rows(slot)], key_ref.at[slot_rows(slot + 1)], core),
-            remote(value_ref.at[:, slot_rows(slot)], value_ref.at[:, slot_rows(slot + 1)], core),
-        ]
-        for slot in (0, 3)
+        share(0, NB, NB),
+        share(2 * NB + HB, HB, 4 * NB + HB),
+        share(3 * NB + HB, HB, 4 * NB),
     ]
     reads = [
         remote(read_w.at[0], read_w.at[slot], peer)
         for slot, peer in ((1, core), (2, far), (3, band), (4, band_core), (5, near))
     ]
-    for c in order:
+    for c in (0, 1):
         to_far[c].start()
-    to_band[0].start()
+    to_band[2].start()
 
     build_enc(enc_src_ref[...], enc_count_ref[...], lat, parity, enc_lo, enc_hi, enc_onehot, enc_pick)
     for copy in grids[:2]:
         copy.wait_recv()
     build_enc(peer_src[...], peer_count[...], lat, parity, enc_lo, enc_hi, enc_onehot, peer_pick)
+    summed = dot(flat_ref[...], enc_pick[0:main, :])
     for copy in grids[2:]:
         copy.wait_recv()
     part_out[...] = dot(flat_ref[...], peer_pick[0:main, :]) + dot(halo_ref[...], peer_pick[main:, :])
-    summed = dot(flat_ref[...], enc_pick[0:main, :]) + dot(halo_ref[...], enc_pick[main:, :])
+    summed = summed + dot(halo_ref[...], enc_pick[main:, :])
     part.start()
-    for c in range(1, CHUNKS):
-        to_band[c].start()
-    to_far[2].wait_recv()
-    on_band[2].start()
-    to_band[0].wait_recv()
+    to_band[3].start()
+    to_band[2].wait_recv()
     on_far[0].start()
     for h in range(HEADS):
         for first, last in ((0, 1), (2, 4), (5, 6)):
             value_ref[h * VROWS + HEAD : (h + 1) * VROWS, first * NB : last * NB] = jnp.ones(
                 (VROWS - HEAD, (last - first) * NB), bf16
             )
-    build_dec(dec_src_ref, lat, lon, inner, dec_pick)
+    build_mask(nbr_ref[...], nbr_count_ref[...], lat, lon, inner, nbr_hi, nbr_lo, nbr_hit, bias_ref)
     part.wait_recv()
-    mean_w[0] = ((summed + part_in[...]) / enc_count_ref[...].astype(f32)).astype(bf16)
-    to_far[3].wait_recv()
-    on_band[3].start()
+    mean = ((summed + part_in[...]) / enc_count_ref[...].astype(f32)).astype(bf16)
+    mean_w[0] = mean[:, :HB]
+    mean_w[1] = mean[:, HB:]
     own_load.wait()
     for copy in means:
         copy.start()
+    for c in (0, 1):
+        to_far[c + 2].start()
+        to_band[c].start()
+    for c in (0, 1):
+        to_far[c].wait_recv()
+        on_band[c].start()
     for load in loads[:4]:
         load.wait()
 
@@ -384,38 +400,36 @@
 
             @pl.when(step == 1)
             def _():
-                to_band[1].wait_recv()
+                to_band[3].wait_recv()
                 on_far[1].start()
+                for copy in means[:2]:
+                    copy.wait_recv()
                 for copy in shares[0]:
                     copy.start()
-                build_mask(nbr_ref[...], nbr_count_ref[...], lat, lon, inner, nbr_hi, nbr_lo, nbr_hit, bias_ref)
-                to_far[0].wait_recv()
-                to_far[1].wait_recv()
-                means[0].wait_recv()
 
             @pl.when(step == 2)
             def _():
-                means[1].wait_recv()
-                to_band[2].wait_recv()
-                to_band[3].wait_recv()
+                for copy in means[2:4] + [to_far[2], to_far[3], to_band[0], to_band[1]]:
+                    copy.wait_recv()
+                for copy in shares[1]:
+                    copy.start()
 
             @pl.when(step == 3)
             def _():
-                for copy in shares[1]:
+                for copy in means[4:] + on_band + on_far:
+                    copy.wait_recv()
+                for copy in shares[2]:
                     copy.start()
-                means[2].wait_recv()
-                for copy in (on_band[2], on_band[3], on_far[0], on_far[1]):
-                    copy.wait_recv()
-
-            slot = 3 * phase + 2 * i
+
+            unit_mean = jnp.concatenate([mean_w[2 * step], mean_w[2 * step + 1]], axis=1)
             embedded = silu(
                 lax.dot_general(
-                    mean_w[slot], w_embed_ref[...], (((0,), (0,)), ((), ())), preferred_element_type=f32
+                    unit_mean, w_embed_ref[...], (((0,), (0,)), ((), ())), preferred_element_type=f32
                 )
             ).astype(bf16)
-            latent = mesh_w[slot].astype(f32) + dot(embedded, weights[0])
+            latent = mesh_w[step].astype(f32) + dot(embedded, weights[0])
             normed = layer_norm(latent, gain_attn_ref[...]).astype(bf16)
-            rows = pl.ds(pl.multiple_of(slot * NB, NB), NB)
+            rows = pl.ds(pl.multiple_of(jnp.where(step == 3, 5, step + jnp.minimum(step, 1)) * NB, NB), NB)
             key_ref[rows, :] = dot(normed, weights[1]).astype(bf16)
             values = dot(normed, weights[2]).T.astype(bf16)
             for h in range(HEADS):
@@ -437,7 +451,7 @@
 
         @pl.when(phase == 1)
         def _():
-            for copy in shares[1]:
+            for copy in shares[1] + shares[2]:
                 copy.wait_recv()
 
         attention(
@@ -478,6 +492,7 @@
     ).astype(bf16)
     for copy in reads:
         copy.start()
+    build_dec(dec_src_ref, lat, lon, inner, dec_pick)
 
     def add_slots(slots, first, last):
         def chunk(c, carry):
@@ -501,8 +516,8 @@
     for copy in reads[1:]:
         copy.wait_recv()
     add_slots((2, 3, 4, 5), False, True)
-    blocks = list(to_far.values()) + to_band + list(on_band.values()) + on_far
-    for copy in grids + [part] + blocks + means + shares[0] + shares[1] + reads:
+    blocks = to_far + list(to_band.values()) + on_band + on_far
+    for copy in grids + [part] + blocks + means + shares[0] + shares[1] + shares[2] + reads:
         copy.wait_send()
 
 
@@ -542,8 +557,8 @@
             pltpu.VMEM((V, NB), f32),
             pltpu.VMEM((V, NB), f32),
             pltpu.VMEM((V, main), f32),
-            pltpu.VMEM((SLOTS, NB, D), bf16),
-            pltpu.VMEM((SLOTS, V, NB), bf16),
+            pltpu.VMEM((4, NB, D), bf16),
+            pltpu.VMEM((8, V, HB), bf16),
             pltpu.VMEM((SLOTS, V, NB), bf16),
             pltpu.VMEM((6, D, D), bf16),
             pltpu.VMEM((KE, NB), f32),

time: 58.9 us -> 57.3 us (0.973)
  Pallas kernels: 56.8 us -> 55.2 us
    pallas_call x1, Pallas kernels: 56.8 us -> 55.2 us  [body(): pl.pallas_call(kernel, out_shape=jax.ShapeDtypeStruct((V, ROWS, COLS), f3...]
where the time goes in v4:
time: 57.3 us; the launch traced here: 57.2 us
  Pallas kernels  55.2 us (96%)
  local copies, waits for them, and re-layouts  1.99 us (3%)
    pallas_call x1, Pallas kernels, body(): pl.pallas_call(kernel, out_shape=jax.ShapeDtypeStruct((V, ROWS, COLS), f3...  55.2 us
    unnamed x1, local copies, waits for them, and re-layouts  1.99 us

profile of v4, /device:TPU:0, one launch (start us, length us, event | category | flops | bytes accessed | tf_op | source)
XLA Modules:
  0.0 57.2 jit_solution(8945893704104161203)
XLA Ops:
  0.0 55.2 %denoise.1 = f32[84,16,128]{2,1,0:T(8,128)} custom-call(bf16[84,16,128]{2,1,0:T(8,128)(2,1)} %grid_ref.1, bf16[256,1024]{1,0:T(8,128)(2,1)} %mesh_ref.1, s32[16,256]{1,0:T(8,128)} %enc_src_ref.1, s32[1,256]{1,0:T(1,128)} %bitcast.8, s32[32,256]{1,0:T(8,128)} %nbr_ref.1, s32[1,256]{1,0:T(1,128)} %bitcast.9, s32[3,16,128]{2,1,0:T(8,128)} %dec_src_ref.1, ...), custom_call_target="tpu_custom_call" | custom-call | tf_op jit(solution)/shard_map/denoise/pallas_call | solution.py:546
  55.2 2.0 %copy.19 = f32[84,16,128]{2,1,0:T(8,128)} copy(f32[84,16,128]{2,1,0:T(8,128)} %denoise.1) | data formatting | bytes 1376256

commit v5 on v4

--- a/solution.py
+++ b/solution.py
@@ -26,6 +26,7 @@
 HB = NB // 2
 HALF = WINDOW // 2
 NEG = -1e30
+VMEM_BYTES = 64 * 1024 * 1024 - 65536 - V * ROWS * COLS * 4 - 8192
 
 
 def tile16(row):
@@ -45,12 +46,12 @@
 
 
 def slot_of(node, lat, lon, inner):
-    member = (node & (NB - 1)).astype(f32)
+    member = node & (NB - 1)
     device = node >> 8
     far = (device >> 6) ^ lat
     sector = device & (SECTORS - 1)
     slot = jnp.where(sector == lon, 3 * far, jnp.where(sector == inner, 1 + 3 * far, 5 - 3 * far))
-    return slot.astype(f32), member
+    return slot, member
 
 
 def pack_grid(grid_ref, flat_ref, edge_ref):
@@ -83,51 +84,51 @@
     hi = jnp.where(halo, 16 + 2 * outer + (r >> 3), r)
     lo = jnp.where(halo, (r & 7) * HALO + c, place - HALO)
     live = (lax.broadcasted_iota(i32, src.shape, 0) < count) & ((row >> 4) == lat)
-    hi_ref[...] = jnp.where(live, hi, -1).astype(f32)
-    lo_ref[...] = lo.astype(f32)
-    iota = row_codes(COLS, NB)
+    hi_ref[...] = jnp.where(live, hi, -1)
+    lo_ref[...] = lo
+    sub = lax.broadcasted_iota(i32, (16, NB), 0)
     for s in range(KE):
-        onehot_ref[s * COLS : (s + 1) * COLS, :] = flag(iota == rep(tile16(lo_ref[s : s + 1, :]), 8))
+        at = jnp.broadcast_to(lo_ref[s : s + 1, :], (16, NB))
+        onehot_ref[s * 16 : (s + 1) * 16, :] = jnp.where((at & 15) == sub, 1 << (4 * (at >> 4)), 0)
 
     def group(g, carry):
-        code = g.astype(f32)
-        acc = jnp.zeros((COLS, NB), bf16)
-        for s in range(KE):
-            hit = tile16(jnp.where(hi_ref[s : s + 1, :] == code, 1.0, 0.0))
-            acc = acc + onehot_ref[s * COLS : (s + 1) * COLS, :] * rep(hit, 8)
-        a_ref[pl.ds(pl.multiple_of(g * COLS, COLS), COLS), :] = acc
+        halves = []
+        for first in (0, KE // 2):
+            acc = jnp.zeros((16, NB), i32)
+            for s in range(first, first + KE // 2):
+                hit = jnp.broadcast_to(hi_ref[s : s + 1, :], (16, NB)) == g
+                acc = acc + jnp.where(hit, onehot_ref[s * 16 : (s + 1) * 16, :], 0)
+            halves.append(acc)
+        even = (halves[0] & 0x0F0F0F0F) + (halves[1] & 0x0F0F0F0F)
+        odd = ((halves[0] >> 4) & 0x0F0F0F0F) + ((halves[1] >> 4) & 0x0F0F0F0F)
+        for k in range(8):
+            counts = ((odd if k % 2 else even) >> (8 * (k // 2))) & 0xFF
+            rows = pl.ds(pl.multiple_of(g * COLS + k * 16, 16), 16)
+            a_ref[rows, :] = counts.astype(f32).astype(bf16)
         return carry
 
     lax.fori_loop(0, 20, group, 0)
 
 
-def build_mask(ids, count, lat, lon, inner, hi_ref, lo_ref, hit_ref, bias_ref):
+def build_mask(ids, count, lat, lon, inner, hi_ref, lo_ref, bias_ref):
     slot, member = slot_of(ids, lat, lon, inner)
     live = lax.broadcasted_iota(i32, ids.shape, 0) < count
-    hi_ref[...] = jnp.where(live, slot, -1.0)
+    hi_ref[...] = jnp.where(live, slot, -1)
     lo_ref[...] = member
+    sub = lax.broadcasted_iota(i32, (8, NB), 0)
+    words = [jnp.zeros((8, NB), i32) for _ in range(SLOTS)]
     for s in range(KM):
+        at = jnp.broadcast_to(lo_ref[s : s + 1, :], (8, NB))
+        where = jnp.broadcast_to(hi_ref[s : s + 1, :], (8, NB))
+        bit = jnp.where((at & 7) == sub, 1 << (at >> 3), 0)
         for b in range(SLOTS):
-            at = (s * SLOTS + b) * 16
-            hit_ref[at : at + 16, :] = tile16(jnp.where(hi_ref[s : s + 1, :] == float(b), 1.0, 0.0))
-    step = 32
-
-    def chunk(c, carry):
-        iota = row_codes(step, NB, c * step)
-        acc = [jnp.zeros((step, NB), bf16) for _ in range(SLOTS)]
-        for s in range(KM):
-            one = flag(iota == rep(tile16(lo_ref[s : s + 1, :]), step // 16))
-            for b in range(SLOTS):
-                at = (s * SLOTS + b) * 16
-                acc[b] = acc[b] + one * rep(hit_ref[at : at + 16, :], step // 16)
-        for b in range(SLOTS):
-            shift = jnp.where(c < NB // step // 2, 0, HB)
-            start = (0, NB, 2 * NB + shift, 3 * NB + HB - 3 * shift, 4 * NB, 5 * NB)[b]
-            rows = pl.ds(pl.multiple_of(start + c * step, step), step)
-            bias_ref[rows, :] = jnp.where(acc[b].astype(f32) > 0.0, 0.0, NEG)
-        return carry
-
-    lax.fori_loop(0, NB // step, chunk, 0)
+            words[b] = words[b] | jnp.where(where == b, bit, 0)
+    for b in range(SLOTS):
+        for k in range(32):
+            late = k >= 16
+            start = (0, NB, 2 * NB + HB * late, 3 * NB + HB - 3 * HB * late, 4 * NB, 5 * NB)[b]
+            seen = (words[b] >> k) & 1
+            bias_ref[start + 8 * k : start + 8 * k + 8, :] = jnp.where(seen == 1, 0.0, NEG)
 
 
 def build_dec(src_ref, lat, lon, inner, pick_ref):
@@ -138,8 +139,8 @@
             for i in range(3):
                 ids = src_ref[i, pl.ds(c * 2 + half, 1), :]
                 slot, member = slot_of(ids, lat, lon, inner)
-                hits = [tile16(jnp.where(slot == float(b), 1.0, 0.0)) for b in range(SLOTS)]
-                codes.append((tile16(member), hits))
+                hits = [tile16(jnp.where(slot == b, 1.0, 0.0)) for b in range(SLOTS)]
+                codes.append((tile16(member.astype(f32)), hits))
             for k in range(4):
                 iota = row_codes(64, COLS, k * 64)
                 ones = [flag(iota == rep(member, 4)) for member, _ in codes]
@@ -210,24 +211,34 @@
 
 
 def kernel(
+    grid_hbm,
+    mesh_ref,
+    enc_src_hbm,
+    enc_count_hbm,
+    nbr_hbm,
+    nbr_count_hbm,
+    dec_src_hbm,
+    w_embed_hbm,
+    w_encode_hbm,
+    w_query_hbm,
+    w_key_hbm,
+    w_value_hbm,
+    w_output_hbm,
+    w_decode_hbm,
+    w_readout_hbm,
+    gain_attn_hbm,
+    gain_dec_hbm,
+    out_ref,
     grid_ref,
-    mesh_ref,
     enc_src_ref,
     enc_count_ref,
     nbr_ref,
     nbr_count_ref,
     dec_src_ref,
     w_embed_ref,
-    w_encode_hbm,
-    w_query_hbm,
-    w_key_hbm,
-    w_value_hbm,
-    w_output_hbm,
-    w_decode_hbm,
     w_readout_ref,
     gain_attn_ref,
     gain_dec_ref,
-    out_ref,
     flat_ref,
     edge_ref,
     halo_ref,
@@ -247,7 +258,6 @@
     peer_pick,
     nbr_hi,
     nbr_lo,
-    nbr_hit,
     bias_ref,
     dec_pick,
     latent_ref,
@@ -284,12 +294,32 @@
     ]
     own_load = pltpu.make_async_copy(mesh_ref, mesh_w.at[0], local_sem.at[6])
 
+    pairs = (
+        (grid_hbm, grid_ref),
+        (enc_src_hbm, enc_src_ref),
+        (enc_count_hbm, enc_count_ref),
+        (nbr_hbm, nbr_ref),
+        (nbr_count_hbm, nbr_count_ref),
+        (dec_src_hbm, dec_src_ref),
+        (w_embed_hbm, w_embed_ref),
+        (gain_attn_hbm, gain_attn_ref),
+        (w_readout_hbm, w_readout_ref),
+        (gain_dec_hbm, gain_dec_ref),
+    )
+    smalls = [
+        pltpu.make_async_copy(source, target, local_sem.at[7 + i])
+        for i, (source, target) in enumerate(pairs)
+    ]
+    for copy in smalls:
+        copy.start()
+
     barrier = pltpu.get_barrier_semaphore()
     for peer in (core, band, band_core, far, near):
         pl.semaphore_signal(barrier, inc=1, device_id=peer, device_id_type=MESH)
     own_load.start()
-    for load in loads:
+    for load in loads[:4]:
         load.start()
+    smalls[0].wait()
     pack_grid(grid_ref, flat_ref, edge_ref)
     pl.semaphore_wait(barrier, 5)
 
@@ -311,8 +341,8 @@
     inner_edge = pl.ds(pl.multiple_of(edge * (1 - parity), edge), edge)
     outer_edge = pl.ds(pl.multiple_of(edge * parity, edge), edge)
     grids = [
-        remote(enc_src_ref, peer_src, band),
-        remote(enc_count_ref, peer_count, band),
+        remote(enc_src_hbm, peer_src, band),
+        remote(enc_count_hbm, peer_count, band),
         remote(edge_ref.at[:, inner_edge], halo_ref.at[:, 0:edge], core),
         remote(edge_ref.at[:, outer_edge], halo_ref.at[:, edge : 2 * edge], near),
     ]
@@ -359,6 +389,8 @@
         to_far[c].start()
     to_band[2].start()
 
+    for copy in smalls[1:3]:
+        copy.wait()
     build_enc(enc_src_ref[...], enc_count_ref[...], lat, parity, enc_lo, enc_hi, enc_onehot, enc_pick)
     for copy in grids[:2]:
         copy.wait_recv()
@@ -377,7 +409,10 @@
             value_ref[h * VROWS + HEAD : (h + 1) * VROWS, first * NB : last * NB] = jnp.ones(
                 (VROWS - HEAD, (last - first) * NB), bf16
             )
-    build_mask(nbr_ref[...], nbr_count_ref[...], lat, lon, inner, nbr_hi, nbr_lo, nbr_hit, bias_ref)
+    for copy in smalls[3:8]:
+        copy.wait()
+    build_mask(nbr_ref[...], nbr_count_ref[...], lat, lon, inner, nbr_hi, nbr_lo, bias_ref)
+    build_dec(dec_src_ref, lat, lon, inner, dec_pick)
     part.wait_recv()
     mean = ((summed + part_in[...]) / enc_count_ref[...].astype(f32)).astype(bf16)
     mean_w[0] = mean[:, :HB]
@@ -391,8 +426,10 @@
     for c in (0, 1):
         to_far[c].wait_recv()
         on_band[c].start()
-    for load in loads[:4]:
+    for load in loads[:3]:
         load.wait()
+    for load in loads[4:]:
+        load.start()
 
     def phase_loop(phase, carry):
         def block(i, carry):
@@ -438,6 +475,7 @@
             @pl.when(step == 0)
             def _():
                 latent_ref[...] = latent
+                loads[3].wait()
                 query_ref[...] = (dot(normed, weights[3]).astype(bf16).astype(f32) * 0.125).astype(bf16)
 
             return carry
@@ -480,7 +518,7 @@
         return carry
 
     lax.fori_loop(0, HEADS, merge, 0)
-    for load in loads[4:]:
+    for load in loads[4:] + smalls[8:]:
         load.wait()
     mixed = latent_ref[...] + lax.dot_general(
         context_ref[...], weights[4], (((0,), (0,)), ((), ())), preferred_element_type=f32
@@ -492,7 +530,6 @@
     ).astype(bf16)
     for copy in reads:
         copy.start()
-    build_dec(dec_src_ref, lat, lon, inner, dec_pick)
 
     def add_slots(slots, first, last):
         def chunk(c, carry):
@@ -545,10 +582,20 @@
     hbm = pl.BlockSpec(memory_space=pl.ANY)
     out = pl.pallas_call(
         kernel,
-        out_shape=jax.ShapeDtypeStruct((V, ROWS, COLS), f32),
-        in_specs=[vmem, hbm] + [vmem] * 6 + [hbm] * 6 + [vmem] * 3,
+        out_shape=pltpu.VMEM((V, ROWS, COLS), f32),
+        in_specs=[hbm] * 17,
         out_specs=vmem,
         scratch_shapes=[
+            pltpu.VMEM((V, ROWS, COLS), bf16),
+            pltpu.VMEM((KE, NB), i32),
+            pltpu.VMEM((1, NB), i32),
+            pltpu.VMEM((KM, NB), i32),
+            pltpu.VMEM((1, NB), i32),
+            pltpu.VMEM((3, ROWS, COLS), i32),
+            pltpu.VMEM((V, D), bf16),
+            pltpu.VMEM((V, D), bf16),
+            pltpu.VMEM((1, D), f32),
+            pltpu.VMEM((1, D), f32),
             pltpu.VMEM((V, main), bf16),
             pltpu.VMEM((V, 2 * ROWS * HALO), bf16),
             pltpu.VMEM((V, 2 * ROWS * HALO), bf16),
@@ -561,14 +608,13 @@
             pltpu.VMEM((8, V, HB), bf16),
             pltpu.VMEM((SLOTS, V, NB), bf16),
             pltpu.VMEM((6, D, D), bf16),
-            pltpu.VMEM((KE, NB), f32),
-            pltpu.VMEM((KE, NB), f32),
-            pltpu.VMEM((KE * COLS, NB), bf16),
+            pltpu.VMEM((KE, NB), i32),
+            pltpu.VMEM((KE, NB), i32),
+            pltpu.VMEM((KE * 16, NB), i32),
             pltpu.VMEM((20 * COLS, NB), bf16),
             pltpu.VMEM((20 * COLS, NB), bf16),
-            pltpu.VMEM((KM, NB), f32),
-            pltpu.VMEM((KM, NB), f32),
-            pltpu.VMEM((KM * SLOTS * 16, NB), bf16),
+            pltpu.VMEM((KM, NB), i32),
+            pltpu.VMEM((KM, NB), i32),
             pltpu.VMEM((WINDOW, NB), f32),
             pltpu.VMEM((8, WINDOW, NB), bf16),
             pltpu.VMEM((NB, D), f32),
@@ -582,12 +628,12 @@
             pltpu.VMEM((2, HEADS, VROWS, NB), f32),
             pltpu.VMEM((2, HEADS, NB), f32),
             pltpu.VMEM((D, NB), bf16),
-            pltpu.SemaphoreType.DMA((7,)),
+            pltpu.SemaphoreType.DMA((17,)),
             pltpu.SemaphoreType.DMA((64,)),
             pltpu.SemaphoreType.DMA((64,)),
         ],
         compiler_params=pltpu.CompilerParams(
-            collective_id=0, has_side_effects=True, vmem_limit_bytes=64 * 1024 * 1024 - 65536
+            collective_id=0, has_side_effects=True, vmem_limit_bytes=VMEM_BYTES
         ),
         name="denoise",
     )(

time: 57.3 us -> 53.5 us (0.934)
  Pallas kernels: 55.2 us -> 52.5 us
  local copies, waits for them, and re-layouts: 1.99 us -> 0.85 us
    pallas_call x1, Pallas kernels: 55.2 us -> 52.5 us  [body(): pl.pallas_call(kernel, out_shape=pltpu.VMEM((V, ROWS, COLS), f32), in_spe...]
    unnamed x1, local copies, waits for them, and re-layouts: 1.99 us -> 0.85 us
where the time goes in v5:
time: 53.5 us; the launch traced here: 53.4 us
  Pallas kernels  52.5 us (98%)
  local copies, waits for them, and re-layouts  0.85 us (2%)
    pallas_call x1, Pallas kernels, body(): pl.pallas_call(kernel, out_shape=pltpu.VMEM((V, ROWS, COLS), f32), in_spe...  52.5 us

profile of v5, /device:TPU:0, one launch (start us, length us, event | category | flops | bytes accessed | tf_op | source)
XLA Modules:
  0.0 53.4 jit_solution(10946097908869383987)
XLA Ops:
  0.0 52.5 %denoise.1 = f32[84,16,128]{2,1,0:T(8,128)S(1)} custom-call(bf16[84,16,128]{2,1,0:T(8,128)(2,1)} %grid_hbm.1, bf16[256,1024]{1,0:T(8,128)(2,1)} %mesh_ref.1, s32[16,256]{1,0:T(8,128)} %enc_src_hbm.1, s32[1,256]{1,0:T(1,128)} %bitcast.8, s32[32,256]{1,0:T(8,128)} %nbr_hbm.1, s32[1,256]{1,0:T(1,128)} %bitcast.9, s32[3,16,128]{2,1,0:T(8,128)} %dec_src_hbm.1, ...), custom_call_target="tpu_custom_call" | custom-call | tf_op jit(solution)/shard_map/denoise/pallas_call | solution.py:583
  52.5 0.8 %copy.19 = f32[84,16,128]{2,1,0:T(8,128)} copy(f32[84,16,128]{2,1,0:T(8,128)S(1)} %denoise.1) | data formatting | bytes 1376256

commit v6 on v5

--- a/solution.py
+++ b/solution.py
@@ -439,10 +439,10 @@
             def _():
                 to_band[3].wait_recv()
                 on_far[1].start()
+                for copy in shares[0]:
+                    copy.start()
                 for copy in means[:2]:
                     copy.wait_recv()
-                for copy in shares[0]:
-                    copy.start()
 
             @pl.when(step == 2)
             def _():
@@ -453,10 +453,11 @@
 
             @pl.when(step == 3)
             def _():
-                for copy in means[4:] + on_band + on_far:
-                    copy.wait_recv()
+                means[4].wait_recv()
                 for copy in shares[2]:
                     copy.start()
+                for copy in on_band + on_far:
+                    copy.wait_recv()
 
             unit_mean = jnp.concatenate([mean_w[2 * step], mean_w[2 * step + 1]], axis=1)
             embedded = silu(

time: 53.5 us -> 53.4 us (level)
  no operation moved by 1% of the time
where the time goes in v6:
time: 53.4 us; the launch traced here: 53.3 us
  Pallas kernels  52.5 us (98%)
  local copies, waits for them, and re-layouts  0.85 us (2%)
    pallas_call x1, Pallas kernels, body(): pl.pallas_call(kernel, out_shape=pltpu.VMEM((V, ROWS, COLS), f32), in_spe...  52.5 us

profile of v6, /device:TPU:0, one launch (start us, length us, event | category | flops | bytes accessed | tf_op | source)
XLA Modules:
  0.0 53.3 jit_solution(14158738411838361096)
XLA Ops:
  0.0 52.5 %denoise.1 = f32[84,16,128]{2,1,0:T(8,128)S(1)} custom-call(bf16[84,16,128]{2,1,0:T(8,128)(2,1)} %grid_hbm.1, bf16[256,1024]{1,0:T(8,128)(2,1)} %mesh_ref.1, s32[16,256]{1,0:T(8,128)} %enc_src_hbm.1, s32[1,256]{1,0:T(1,128)} %bitcast.8, s32[32,256]{1,0:T(8,128)} %nbr_hbm.1, s32[1,256]{1,0:T(1,128)} %bitcast.9, s32[3,16,128]{2,1,0:T(8,128)} %dec_src_hbm.1, ...), custom_call_target="tpu_custom_call" | custom-call | tf_op jit(solution)/shard_map/denoise/pallas_call | solution.py:584
  52.5 0.8 %copy.19 = f32[84,16,128]{2,1,0:T(8,128)} copy(f32[84,16,128]{2,1,0:T(8,128)S(1)} %denoise.1) | data formatting | bytes 1376256
